TPU v7x, 512 devices: a whole 4x8x8 slice. The times are simulated.
512 devices in a mesh: ctx: 64 (over z_hi, y, core), head: 8 (over z_lo, x).
Axes of the slice: x: 4, y: 8, z: 8 (z_hi: 4, z_lo: 2; z = z_hi * 2 + z_lo), core: 2. Of those that a mesh axis runs over, the one named last changes fastest.
Arguments:
- queries: bfloat16 [3072, 8192], P('ctx', 'head'), may hold values from -120 to 120
- cached_keys: bfloat16 [20480, 1024], P('ctx', 'head'), may hold values from -5 to 15
- cached_values: bfloat16 [20480, 1024], P('ctx', 'head'), may hold values from -6 to 6
- fresh_keys: bfloat16 [3072, 1024], P('ctx', 'head'), may hold values from -5 to 15
- fresh_values: bfloat16 [3072, 1024], P('ctx', 'head'), may hold values from -6 to 6
- recompute_index: int32 [64, 48], P('ctx'), may hold values from 0 to 319, as said below
- recompute_count: int32 [64], P('ctx'), may hold values from 1 to 48, 2688 in all
- group_offsets: int32 [64], replicated, may hold values from 0 to 40257, as said below
Outputs:
- attention: bfloat16 [3072, 8192], P('ctx', 'head')
- joined_keys: bfloat16 [20480, 1024], P('ctx', 'head')
- joined_values: bfloat16 [20480, 1024], P('ctx', 'head')
- drift: float32 [64, 48], P('ctx')
Inputs may be any that keep to these rules, and one draw needn't show every extreme that they name: `recompute_index`: the entries of one group's row are different token numbers of that group. group_offsets[c + 1] - group_offsets[c] lies between 320 and 639.
All inputs are finite; a program needn't handle non-finite values. No bound on the sum of `recompute_count` on one device may be relied on, other than what follows from the above.
Results may differ from a plain program's by a relative error of at most 0.008.
Values may be sent and summed in bfloat16 or wider, within the bound.
No kernel may reach another device: no remote copies, remote signals or barrier semaphores. Data moves between devices by JAX's collectives and lax.ppermute only.
A program may use at most 64 MiB of HBM per device.

v0:
```python
import math

import jax
import jax.numpy as jnp
from jax import lax
from jax.sharding import PartitionSpec as P

HEADS = 64
KV_HEADS = 8
HEAD_DIM = 128


NEG_FILL = -1e30
BLOCK_TOKENS = 2560


def sent_to_all(value, axis):
    size = lax.axis_size(axis)
    return lax.all_to_all(
        jnp.broadcast_to(value[None], (size, *value.shape)), axis, 0, 0, tiled=True
    )


def over_copies(value, axis):
    return sent_to_all(value, axis).sum(axis=0)


def side_by_side(arrays, axis, dim, along):
    ends, at = ([], 0)
    for a in arrays[:-1]:
        at += a.shape[along]
        ends.append(at)
    both = jnp.concatenate(arrays, axis=along)
    return tuple(jnp.split(lax.all_gather(both, axis, axis=dim, tiled=True), ends, axis=along))


def inverse_freq():
    half_dim = HEAD_DIM // 2
    exponent = jnp.arange(half_dim, dtype=jnp.float32) * 2.0 / HEAD_DIM
    base_freq = 1.0 / 500000.0**exponent
    wavelength = 2.0 * jnp.pi / base_freq
    smooth = (8192.0 / wavelength - 1.0) / 3.0
    blended_freq = (1.0 - smooth) * base_freq / 8.0 + smooth * base_freq
    return jnp.where(
        wavelength < 2048.0,
        base_freq,
        jnp.where(wavelength > 8192.0, base_freq / 8.0, blended_freq),
    )


def rotate(values, positions):
    row_count = values.shape[0]
    head_count = values.shape[1] // HEAD_DIM
    half_dim = HEAD_DIM // 2
    angles = positions.astype(jnp.float32)[:, None] * inverse_freq()[None, :]
    cosine = jnp.cos(angles)[:, None, :]
    sine_part = jnp.sin(angles)[:, None, :]
    pieces_f = values.astype(jnp.float32).reshape(row_count, head_count, HEAD_DIM)
    first_half = pieces_f[:, :, :half_dim]
    second_half = pieces_f[:, :, half_dim:]
    turned = jnp.concatenate(
        [
            first_half * cosine - second_half * sine_part,
            second_half * cosine + first_half * sine_part,
        ],
        axis=2,
    )
    return turned.reshape(row_count, head_count * HEAD_DIM)


def empty_state(kv_local, row_count):
    return (
        jnp.full((kv_local, row_count), NEG_FILL, jnp.float32),
        jnp.zeros((kv_local, row_count), jnp.float32),
        jnp.zeros((kv_local, row_count, HEAD_DIM), jnp.float32),
    )


def attend(status, queries, query_pos, key_rows, value_rows, key_pos):
    maxima, totals, weighted = status
    scores = jnp.einsum("hqd,khd->hqk", queries, key_rows, preferred_element_type=jnp.float32) * (
        1.0 / math.sqrt(HEAD_DIM)
    )
    visible = key_pos[None, None, :] <= query_pos[None, :, None]
    block_peak = jnp.max(jnp.where(visible, scores, NEG_FILL), axis=2)
    raised = jnp.maximum(maxima, block_peak)
    weights = jnp.where(visible, jnp.exp(scores - raised[:, :, None]), 0.0)
    shrink = jnp.exp(maxima - raised)
    totals = totals * shrink + jnp.sum(weights, axis=2)
    weighted = weighted * shrink[:, :, None] + jnp.einsum(
        "hqk,khd->hqd", weights.astype(jnp.bfloat16), value_rows, preferred_element_type=jnp.float32
    )
    return (raised, totals, weighted)


def finish(status, tokens, heads_per):
    weighted = status[2]
    kv_local = weighted.shape[0]
    normalized = weighted / status[1][:, :, None]
    return (
        normalized.reshape(kv_local, tokens, heads_per, HEAD_DIM)
        .transpose(1, 0, 2, 3)
        .reshape(tokens, kv_local * heads_per * HEAD_DIM)
    )


def block_groups(groups_in, group_len):
    best = 1
    for count in range(1, groups_in + 1):
        if groups_in % count == 0 and count * group_len <= max(BLOCK_TOKENS, group_len):
            best = count
    return best


def fold_keys(group_offsets, group_len, query_sets):

    def absorb(running, piece, start):
        key_rows, value_rows = piece
        row_count = key_rows.shape[0]
        kv_local = key_rows.shape[1] // HEAD_DIM
        groups_in = row_count // group_len
        groups_each = block_groups(groups_in, group_len)
        block_count = groups_in // groups_each
        key_blocks = key_rows.reshape(block_count, groups_each * group_len, kv_local, HEAD_DIM)
        value_blocks = value_rows.reshape(block_count, groups_each * group_len, kv_local, HEAD_DIM)
        first_group = start // group_len

        def advance(current_states, block_item):
            key_block, value_block, number = block_item
            lead_group = number * groups_each
            group_starts = lax.dynamic_slice_in_dim(group_offsets, lead_group, groups_each)
            key_pos = (
                group_starts[:, None] + jnp.arange(group_len, dtype=jnp.int32)[None, :]
            ).reshape(-1)
            updated = []
            for status, query_set in zip(current_states, query_sets):
                updated.append(
                    lax.cond(
                        lead_group <= query_set[2],
                        lambda current: attend(
                            current, query_set[0], query_set[1], key_block, value_block, key_pos
                        ),
                        lambda current: current,
                        status,
                    )
                )
            return (tuple(updated), None)

        result_states, _ = lax.scan(
            advance, running, (key_blocks, value_blocks, jnp.arange(block_count, dtype=jnp.int32))
        )
        return result_states

    return absorb


def shards(
    queries,
    cached_keys,
    cached_values,
    fresh_keys,
    fresh_values,
    recompute_index,
    recompute_count,
    group_offsets,
):
    group_len = cached_keys.shape[0]
    rows_dev = queries.shape[0]
    kv_local = cached_keys.shape[1] // HEAD_DIM
    heads_per = HEADS // KV_HEADS
    own_group = lax.axis_index("ctx")
    own_start = lax.dynamic_index_in_dim(group_offsets, own_group, keepdims=False)
    indices = recompute_index[0]
    live_rows = jnp.arange(rows_dev, dtype=jnp.int32) < recompute_count[0]
    turned = rotate(cached_keys, own_start + jnp.zeros((group_len,), jnp.int32)).astype(
        jnp.bfloat16
    )
    fresh_turned = rotate(fresh_keys, own_start + indices).astype(jnp.bfloat16)
    picker = (jnp.arange(group_len, dtype=jnp.int32)[:, None] == indices[None, :]) & live_rows[
        None, :
    ]
    covered = jnp.any(picker, axis=1)[:, None]
    picker = picker.astype(jnp.bfloat16)
    joined_keys = jnp.where(
        covered,
        jnp.dot(picker, fresh_turned, preferred_element_type=jnp.float32),
        turned.astype(jnp.float32),
    ).astype(jnp.bfloat16)
    joined_values = jnp.where(
        covered,
        jnp.dot(picker, fresh_values, preferred_element_type=jnp.float32),
        cached_values.astype(jnp.float32),
    ).astype(jnp.bfloat16)
    key_gap = fresh_turned.astype(jnp.float32) - jnp.take(turned, indices, axis=0).astype(
        jnp.float32
    )
    value_gap = fresh_values.astype(jnp.float32) - jnp.take(cached_values, indices, axis=0).astype(
        jnp.float32
    )
    local_drift = jnp.sum(key_gap * key_gap + value_gap * value_gap, axis=1)
    kv_drift = over_copies(local_drift, "head") / (2.0 * KV_HEADS * HEAD_DIM)
    kv_drift = jnp.where(live_rows, kv_drift, 0.0)[None, :]
    query_pos = own_start + indices
    turned_queries = rotate(queries, query_pos).astype(jnp.bfloat16)
    query_grid = (
        turned_queries.reshape(rows_dev, kv_local, heads_per, HEAD_DIM)
        .transpose(1, 0, 2, 3)
        .reshape(kv_local, rows_dev * heads_per, HEAD_DIM)
    )
    grid_pos = jnp.repeat(query_pos, heads_per)
    absorb = fold_keys(group_offsets, group_len, ((query_grid, grid_pos, own_group),))
    (own_state,) = absorb(
        (empty_state(kv_local, rows_dev * heads_per),),
        side_by_side((joined_keys, joined_values), "ctx", 0, 1),
        jnp.int32(0),
    )
    attended = finish(own_state, rows_dev, heads_per).astype(jnp.bfloat16)
    attention = jnp.where(live_rows[:, None], attended, jnp.zeros((), jnp.bfloat16))
    return (attention, joined_keys, joined_values, kv_drift)


def solution(mesh):
    return jax.shard_map(
        shards,
        mesh=mesh,
        in_specs=(
            P("ctx", "head"),
            P("ctx", "head"),
            P("ctx", "head"),
            P("ctx", "head"),
            P("ctx", "head"),
            P("ctx", None),
            P("ctx"),
            P(),
        ),
        out_specs=(P("ctx", "head"), P("ctx", "head"), P("ctx", "head"), P("ctx", None)),
        check_vma=False,
    )
```

profile of v0, /device:TPU:441, one launch (start us, length us, event | category | flops | bytes accessed | tf_op | source)
XLA Modules:
  0.0 206.8 jit_solution(5435910337130421964)
XLA Ops:
  9.9 1.3 fusion.43
  16.9 1.5 gather_fusion.1
  21.2 4.9 %all-to-all-start = ((f32[8,1,48]{2,1,0:T(1,128)}), f32[8,1,48]{2,1,0:T(1,128)S(1)}, u32[]{:S(2)}, u32[]{:S(2)}) async-start(f32[8,1,48]{2,1,0:T(1,128)} %broadcast_in_dim.90), calls=%async_computation | async-start | bytes 8192 | tf_op jit(solution)/shard_map/all_to_all | solution.py:19
  27.5 3.6 %all-to-all-done = f32[8,1,48]{2,1,0:T(1,128)S(1)} async-done(((f32[8,1,48]{2,1,0:T(1,128)}), f32[8,1,48]{2,1,0:T(1,128)S(1)}, u32[]{:S(2)}, u32[]{:S(2)}) %all-to-all-start) | async-done | bytes 1568 | tf_op jit(solution)/shard_map/all_to_all | solution.py:19
  31.6 94.8 %all-gather.2.cloned.1.call-done = bf16[20480,256]{1,0:T(8,128)(2,1)} async-done(((bf16[320,256]{1,0:T(8,128)(2,1)}), bf16[20480,256]{1,0:T(8,128)(2,1)}) %all-gather.2.cloned.1.call-update) | async-done | bytes 10485776 | tf_op jit(solution)/shard_map/all_gather | solution.py:34
  126.4 8.9 %fusion.44 = (bf16[20480,128]{1,0:T(8,128)(2,1)}, bf16[20480,128]{1,0:T(8,128)(2,1)}) fusion(bf16[20480,256]{1,0:T(8,128)(2,1)} %all-gather.2.cloned.1.call-done), kind=kLoop, calls=%fused_computation.76 | loop fusion | bytes 20971520 | tf_op jit(solution)/shard_map/split | solution.py:34
  135.3 63.7 %while.15 = (s32[]{:T(128)}, f32[1,384]{1,0:T(1,128)S(1)}, f32[1,384]{1,0:T(1,128)S(1)}, f32[1,384,128]{2,1,0:T(8,128)S(1)}, s32[8]{0:T(128)S(1)}, /*index=5*/s3...) while((s32[]{:T(128)}, f32[1,384]{1,0:T(1,128)S(1)}, ...), condition=%wide.region_6.7_spmd.clone, body=%wide.region_1.0_spmd.clone.sunk | while | flops 515214976 | bytes 13717633 | solution.py:149
  136.5 6.8 %conditional.3 = ((f32[1,384]{1,0:T(1,128)S(1)}, f32[1,384]{1,0:T(1,128)S(1)}, f32[1,384,128]{2,1,0:T(8,128)S(1)})) conditional(s32[]{:T(128)} %convert_element_type.107, (f32[1,384]{1,0:T(1,128)S(1)}, f32[1,384]{1,0:T(1,128)S(1)}, f32[1,384,128]{2,1,0:T(8,128)S(1)}) %tuple.58, (s32[]{:T(128)}, s32[64]{0:T(128)S(1)}, s32[8,320]{1,0:T(8,128)S(1)}, ...), branch_computations={%region_2.2_spmd, %region_3.5_spmd} | conditional | flops 515214976 | bytes 13707110 | solution.py:138
  136.9 2.5 %fusion.3 = (f32[384]{0:T(512)S(1)}, f32[384,2560]{0,1:T(8,128)S(1)}) fusion(s32[384]{0:T(512)S(1)} %le.24, s32[2560]{0:T(1024)S(1)} %le.22, bf16[1,384,128]{2,1,0:T(8,128)(2,1)S(1)} %get-tuple-element.154, bf16[8,2560,1,128]{3,1,2,0:T(8,128)(2,1)} %get-tuple-element.152, s32[]{:T(128)} %get-tuple-element.153), kind=kOutput, calls=%fused_computation.7 | convolution fusion | flops 255590016 | bytes 4699648 | tf_op jit(solution)/shard_map/while/body/eval_jaxpr/cond/branch_1_fun/hqd,khd->hqk/dot_general | solution.py:81
  139.5 2.5 %fusion.12 = f32[1,384,128]{2,1,0:T(8,128)S(1)} fusion(f32[384,2560]{0,1:T(8,128)S(1)} %get-tuple-element.282, f32[384]{0:T(512)S(1)} %get-tuple-element.255, s32[384]{0:T(512)S(1)} %le.24, s32[2560]{0:T(1024)S(1)} %le.22, bf16[8,2560,1,128]{3,1,2,0:T(8,128)(2,1)} %get-tuple-element.157, s32[]{:T(128)} %get-tuple-element.153, ...), kind=kOutput, calls=%fused_computation.13 | convolution fusion | flops 255688704 | bytes 4996096 | tf_op jit(solution)/shard_map/while/body/eval_jaxpr/cond/branch_1_fun/hqk,khd->hqd/dot_general | solution.py:90
  142.0 1.3 fusion.5
  144.4 6.8 %conditional.3 = ((f32[1,384]{1,0:T(1,128)S(1)}, f32[1,384]{1,0:T(1,128)S(1)}, f32[1,384,128]{2,1,0:T(8,128)S(1)})) conditional(s32[]{:T(128)} %convert_element_type.107, (f32[1,384]{1,0:T(1,128)S(1)}, f32[1,384]{1,0:T(1,128)S(1)}, f32[1,384,128]{2,1,0:T(8,128)S(1)}) %tuple.58, (s32[]{:T(128)}, s32[64]{0:T(128)S(1)}, s32[8,320]{1,0:T(8,128)S(1)}, ...), branch_computations={%region_2.2_spmd, %region_3.5_spmd} | conditional | flops 515214976 | bytes 13707110 | solution.py:138
  144.9 2.5 %fusion.3 = (f32[384]{0:T(512)S(1)}, f32[384,2560]{0,1:T(8,128)S(1)}) fusion(s32[384]{0:T(512)S(1)} %le.24, s32[2560]{0:T(1024)S(1)} %le.22, bf16[1,384,128]{2,1,0:T(8,128)(2,1)S(1)} %get-tuple-element.154, bf16[8,2560,1,128]{3,1,2,0:T(8,128)(2,1)} %get-tuple-element.152, s32[]{:T(128)} %get-tuple-element.153), kind=kOutput, calls=%fused_computation.7 | convolution fusion | flops 255590016 | bytes 4699648 | tf_op jit(solution)/shard_map/while/body/eval_jaxpr/cond/branch_1_fun/hqd,khd->hqk/dot_general | solution.py:81
  147.4 2.5 %fusion.12 = f32[1,384,128]{2,1,0:T(8,128)S(1)} fusion(f32[384,2560]{0,1:T(8,128)S(1)} %get-tuple-element.282, f32[384]{0:T(512)S(1)} %get-tuple-element.255, s32[384]{0:T(512)S(1)} %le.24, s32[2560]{0:T(1024)S(1)} %le.22, bf16[8,2560,1,128]{3,1,2,0:T(8,128)(2,1)} %get-tuple-element.157, s32[]{:T(128)} %get-tuple-element.153, ...), kind=kOutput, calls=%fused_computation.13 | convolution fusion | flops 255688704 | bytes 4996096 | tf_op jit(solution)/shard_map/while/body/eval_jaxpr/cond/branch_1_fun/hqk,khd->hqd/dot_general | solution.py:90
  152.4 6.8 %conditional.3 = ((f32[1,384]{1,0:T(1,128)S(1)}, f32[1,384]{1,0:T(1,128)S(1)}, f32[1,384,128]{2,1,0:T(8,128)S(1)})) conditional(s32[]{:T(128)} %convert_element_type.107, (f32[1,384]{1,0:T(1,128)S(1)}, f32[1,384]{1,0:T(1,128)S(1)}, f32[1,384,128]{2,1,0:T(8,128)S(1)}) %tuple.58, (s32[]{:T(128)}, s32[64]{0:T(128)S(1)}, s32[8,320]{1,0:T(8,128)S(1)}, ...), branch_computations={%region_2.2_spmd, %region_3.5_spmd} | conditional | flops 515214976 | bytes 13707110 | solution.py:138
  152.8 2.5 %fusion.3 = (f32[384]{0:T(512)S(1)}, f32[384,2560]{0,1:T(8,128)S(1)}) fusion(s32[384]{0:T(512)S(1)} %le.24, s32[2560]{0:T(1024)S(1)} %le.22, bf16[1,384,128]{2,1,0:T(8,128)(2,1)S(1)} %get-tuple-element.154, bf16[8,2560,1,128]{3,1,2,0:T(8,128)(2,1)} %get-tuple-element.152, s32[]{:T(128)} %get-tuple-element.153), kind=kOutput, calls=%fused_computation.7 | convolution fusion | flops 255590016 | bytes 4699648 | tf_op jit(solution)/shard_map/while/body/eval_jaxpr/cond/branch_1_fun/hqd,khd->hqk/dot_general | solution.py:81
  155.4 2.5 %fusion.12 = f32[1,384,128]{2,1,0:T(8,128)S(1)} fusion(f32[384,2560]{0,1:T(8,128)S(1)} %get-tuple-element.282, f32[384]{0:T(512)S(1)} %get-tuple-element.255, s32[384]{0:T(512)S(1)} %le.24, s32[2560]{0:T(1024)S(1)} %le.22, bf16[8,2560,1,128]{3,1,2,0:T(8,128)(2,1)} %get-tuple-element.157, s32[]{:T(128)} %get-tuple-element.153, ...), kind=kOutput, calls=%fused_computation.13 | convolution fusion | flops 255688704 | bytes 4996096 | tf_op jit(solution)/shard_map/while/body/eval_jaxpr/cond/branch_1_fun/hqk,khd->hqd/dot_general | solution.py:90
  160.4 6.8 %conditional.3 = ((f32[1,384]{1,0:T(1,128)S(1)}, f32[1,384]{1,0:T(1,128)S(1)}, f32[1,384,128]{2,1,0:T(8,128)S(1)})) conditional(s32[]{:T(128)} %convert_element_type.107, (f32[1,384]{1,0:T(1,128)S(1)}, f32[1,384]{1,0:T(1,128)S(1)}, f32[1,384,128]{2,1,0:T(8,128)S(1)}) %tuple.58, (s32[]{:T(128)}, s32[64]{0:T(128)S(1)}, s32[8,320]{1,0:T(8,128)S(1)}, ...), branch_computations={%region_2.2_spmd, %region_3.5_spmd} | conditional | flops 515214976 | bytes 13707110 | solution.py:138
  160.8 2.5 %fusion.3 = (f32[384]{0:T(512)S(1)}, f32[384,2560]{0,1:T(8,128)S(1)}) fusion(s32[384]{0:T(512)S(1)} %le.24, s32[2560]{0:T(1024)S(1)} %le.22, bf16[1,384,128]{2,1,0:T(8,128)(2,1)S(1)} %get-tuple-element.154, bf16[8,2560,1,128]{3,1,2,0:T(8,128)(2,1)} %get-tuple-element.152, s32[]{:T(128)} %get-tuple-element.153), kind=kOutput, calls=%fused_computation.7 | convolution fusion | flops 255590016 | bytes 4699648 | tf_op jit(solution)/shard_map/while/body/eval_jaxpr/cond/branch_1_fun/hqd,khd->hqk/dot_general | solution.py:81
  163.4 2.5 %fusion.12 = f32[1,384,128]{2,1,0:T(8,128)S(1)} fusion(f32[384,2560]{0,1:T(8,128)S(1)} %get-tuple-element.282, f32[384]{0:T(512)S(1)} %get-tuple-element.255, s32[384]{0:T(512)S(1)} %le.24, s32[2560]{0:T(1024)S(1)} %le.22, bf16[8,2560,1,128]{3,1,2,0:T(8,128)(2,1)} %get-tuple-element.157, s32[]{:T(128)} %get-tuple-element.153, ...), kind=kOutput, calls=%fused_computation.13 | convolution fusion | flops 255688704 | bytes 4996096 | tf_op jit(solution)/shard_map/while/body/eval_jaxpr/cond/branch_1_fun/hqk,khd->hqd/dot_general | solution.py:90
  168.3 6.8 %conditional.3 = ((f32[1,384]{1,0:T(1,128)S(1)}, f32[1,384]{1,0:T(1,128)S(1)}, f32[1,384,128]{2,1,0:T(8,128)S(1)})) conditional(s32[]{:T(128)} %convert_element_type.107, (f32[1,384]{1,0:T(1,128)S(1)}, f32[1,384]{1,0:T(1,128)S(1)}, f32[1,384,128]{2,1,0:T(8,128)S(1)}) %tuple.58, (s32[]{:T(128)}, s32[64]{0:T(128)S(1)}, s32[8,320]{1,0:T(8,128)S(1)}, ...), branch_computations={%region_2.2_spmd, %region_3.5_spmd} | conditional | flops 515214976 | bytes 13707110 | solution.py:138
  168.7 2.5 %fusion.3 = (f32[384]{0:T(512)S(1)}, f32[384,2560]{0,1:T(8,128)S(1)}) fusion(s32[384]{0:T(512)S(1)} %le.24, s32[2560]{0:T(1024)S(1)} %le.22, bf16[1,384,128]{2,1,0:T(8,128)(2,1)S(1)} %get-tuple-element.154, bf16[8,2560,1,128]{3,1,2,0:T(8,128)(2,1)} %get-tuple-element.152, s32[]{:T(128)} %get-tuple-element.153), kind=kOutput, calls=%fused_computation.7 | convolution fusion | flops 255590016 | bytes 4699648 | tf_op jit(solution)/shard_map/while/body/eval_jaxpr/cond/branch_1_fun/hqd,khd->hqk/dot_general | solution.py:81
  171.3 2.5 %fusion.12 = f32[1,384,128]{2,1,0:T(8,128)S(1)} fusion(f32[384,2560]{0,1:T(8,128)S(1)} %get-tuple-element.282, f32[384]{0:T(512)S(1)} %get-tuple-element.255, s32[384]{0:T(512)S(1)} %le.24, s32[2560]{0:T(1024)S(1)} %le.22, bf16[8,2560,1,128]{3,1,2,0:T(8,128)(2,1)} %get-tuple-element.157, s32[]{:T(128)} %get-tuple-element.153, ...), kind=kOutput, calls=%fused_computation.13 | convolution fusion | flops 255688704 | bytes 4996096 | tf_op jit(solution)/shard_map/while/body/eval_jaxpr/cond/branch_1_fun/hqk,khd->hqd/dot_general | solution.py:90
  176.3 6.8 %conditional.3 = ((f32[1,384]{1,0:T(1,128)S(1)}, f32[1,384]{1,0:T(1,128)S(1)}, f32[1,384,128]{2,1,0:T(8,128)S(1)})) conditional(s32[]{:T(128)} %convert_element_type.107, (f32[1,384]{1,0:T(1,128)S(1)}, f32[1,384]{1,0:T(1,128)S(1)}, f32[1,384,128]{2,1,0:T(8,128)S(1)}) %tuple.58, (s32[]{:T(128)}, s32[64]{0:T(128)S(1)}, s32[8,320]{1,0:T(8,128)S(1)}, ...), branch_computations={%region_2.2_spmd, %region_3.5_spmd} | conditional | flops 515214976 | bytes 13707110 | solution.py:138
  176.7 2.5 %fusion.3 = (f32[384]{0:T(512)S(1)}, f32[384,2560]{0,1:T(8,128)S(1)}) fusion(s32[384]{0:T(512)S(1)} %le.24, s32[2560]{0:T(1024)S(1)} %le.22, bf16[1,384,128]{2,1,0:T(8,128)(2,1)S(1)} %get-tuple-element.154, bf16[8,2560,1,128]{3,1,2,0:T(8,128)(2,1)} %get-tuple-element.152, s32[]{:T(128)} %get-tuple-element.153), kind=kOutput, calls=%fused_computation.7 | convolution fusion | flops 255590016 | bytes 4699648 | tf_op jit(solution)/shard_map/while/body/eval_jaxpr/cond/branch_1_fun/hqd,khd->hqk/dot_general | solution.py:81
  179.3 2.5 %fusion.12 = f32[1,384,128]{2,1,0:T(8,128)S(1)} fusion(f32[384,2560]{0,1:T(8,128)S(1)} %get-tuple-element.282, f32[384]{0:T(512)S(1)} %get-tuple-element.255, s32[384]{0:T(512)S(1)} %le.24, s32[2560]{0:T(1024)S(1)} %le.22, bf16[8,2560,1,128]{3,1,2,0:T(8,128)(2,1)} %get-tuple-element.157, s32[]{:T(128)} %get-tuple-element.153, ...), kind=kOutput, calls=%fused_computation.13 | convolution fusion | flops 255688704 | bytes 4996096 | tf_op jit(solution)/shard_map/while/body/eval_jaxpr/cond/branch_1_fun/hqk,khd->hqd/dot_general | solution.py:90
  184.2 6.8 %conditional.3 = ((f32[1,384]{1,0:T(1,128)S(1)}, f32[1,384]{1,0:T(1,128)S(1)}, f32[1,384,128]{2,1,0:T(8,128)S(1)})) conditional(s32[]{:T(128)} %convert_element_type.107, (f32[1,384]{1,0:T(1,128)S(1)}, f32[1,384]{1,0:T(1,128)S(1)}, f32[1,384,128]{2,1,0:T(8,128)S(1)}) %tuple.58, (s32[]{:T(128)}, s32[64]{0:T(128)S(1)}, s32[8,320]{1,0:T(8,128)S(1)}, ...), branch_computations={%region_2.2_spmd, %region_3.5_spmd} | conditional | flops 515214976 | bytes 13707110 | solution.py:138
  184.7 2.5 %fusion.3 = (f32[384]{0:T(512)S(1)}, f32[384,2560]{0,1:T(8,128)S(1)}) fusion(s32[384]{0:T(512)S(1)} %le.24, s32[2560]{0:T(1024)S(1)} %le.22, bf16[1,384,128]{2,1,0:T(8,128)(2,1)S(1)} %get-tuple-element.154, bf16[8,2560,1,128]{3,1,2,0:T(8,128)(2,1)} %get-tuple-element.152, s32[]{:T(128)} %get-tuple-element.153), kind=kOutput, calls=%fused_computation.7 | convolution fusion | flops 255590016 | bytes 4699648 | tf_op jit(solution)/shard_map/while/body/eval_jaxpr/cond/branch_1_fun/hqd,khd->hqk/dot_general | solution.py:81
  187.2 2.5 %fusion.12 = f32[1,384,128]{2,1,0:T(8,128)S(1)} fusion(f32[384,2560]{0,1:T(8,128)S(1)} %get-tuple-element.282, f32[384]{0:T(512)S(1)} %get-tuple-element.255, s32[384]{0:T(512)S(1)} %le.24, s32[2560]{0:T(1024)S(1)} %le.22, bf16[8,2560,1,128]{3,1,2,0:T(8,128)(2,1)} %get-tuple-element.157, s32[]{:T(128)} %get-tuple-element.153, ...), kind=kOutput, calls=%fused_computation.13 | convolution fusion | flops 255688704 | bytes 4996096 | tf_op jit(solution)/shard_map/while/body/eval_jaxpr/cond/branch_1_fun/hqk,khd->hqd/dot_general | solution.py:90
  192.2 6.8 %conditional.3 = ((f32[1,384]{1,0:T(1,128)S(1)}, f32[1,384]{1,0:T(1,128)S(1)}, f32[1,384,128]{2,1,0:T(8,128)S(1)})) conditional(s32[]{:T(128)} %convert_element_type.107, (f32[1,384]{1,0:T(1,128)S(1)}, f32[1,384]{1,0:T(1,128)S(1)}, f32[1,384,128]{2,1,0:T(8,128)S(1)}) %tuple.58, (s32[]{:T(128)}, s32[64]{0:T(128)S(1)}, s32[8,320]{1,0:T(8,128)S(1)}, ...), branch_computations={%region_2.2_spmd, %region_3.5_spmd} | conditional | flops 515214976 | bytes 13707110 | solution.py:138
  192.6 2.5 %fusion.3 = (f32[384]{0:T(512)S(1)}, f32[384,2560]{0,1:T(8,128)S(1)}) fusion(s32[384]{0:T(512)S(1)} %le.24, s32[2560]{0:T(1024)S(1)} %le.22, bf16[1,384,128]{2,1,0:T(8,128)(2,1)S(1)} %get-tuple-element.154, bf16[8,2560,1,128]{3,1,2,0:T(8,128)(2,1)} %get-tuple-element.152, s32[]{:T(128)} %get-tuple-element.153), kind=kOutput, calls=%fused_computation.7 | convolution fusion | flops 255590016 | bytes 4699648 | tf_op jit(solution)/shard_map/while/body/eval_jaxpr/cond/branch_1_fun/hqd,khd->hqk/dot_general | solution.py:81
  195.2 2.5 %fusion.12 = f32[1,384,128]{2,1,0:T(8,128)S(1)} fusion(f32[384,2560]{0,1:T(8,128)S(1)} %get-tuple-element.282, f32[384]{0:T(512)S(1)} %get-tuple-element.255, s32[384]{0:T(512)S(1)} %le.24, s32[2560]{0:T(1024)S(1)} %le.22, bf16[8,2560,1,128]{3,1,2,0:T(8,128)(2,1)} %get-tuple-element.157, s32[]{:T(128)} %get-tuple-element.153, ...), kind=kOutput, calls=%fused_computation.13 | convolution fusion | flops 255688704 | bytes 4996096 | tf_op jit(solution)/shard_map/while/body/eval_jaxpr/cond/branch_1_fun/hqk,khd->hqd/dot_general | solution.py:90
  (128 shorter events, 29.6 us)
Async XLA Ops:
  7.2 119.2 %all-gather.2.cloned.1.call-start = ((), (), s32[]{:S(2)}) async-start(), calls=%async_computation.1 | async-start | bytes 10649600 | tf_op jit(solution)/shard_map/all_gather | solution.py:34
  15.2 120.1 %copy-start = (bf16[320,128]{1,0:T(8,128)(2,1)}, bf16[320,128]{1,0:T(8,128)(2,1)S(1)}, u32[]{:S(2)}) copy-start(bf16[320,128]{1,0:T(8,128)(2,1)S(1)} %fusion.25) | copy-start | bytes 245764
  16.2 119.1 %copy-start.1 = (bf16[320,128]{1,0:T(8,128)(2,1)}, bf16[320,128]{1,0:T(8,128)(2,1)S(1)}, u32[]{:S(2)}) copy-start(bf16[320,128]{1,0:T(8,128)(2,1)S(1)} %fusion.24) | copy-start | bytes 245764
  21.2 9.9 %all-to-all-start = ((f32[8,1,48]{2,1,0:T(1,128)}), f32[8,1,48]{2,1,0:T(1,128)S(1)}, u32[]{:S(2)}, u32[]{:S(2)}) async-start(f32[8,1,48]{2,1,0:T(1,128)} %broadcast_in_dim.90), calls=%async_computation | async-start | bytes 8192 | tf_op jit(solution)/shard_map/all_to_all | solution.py:19
  31.6 103.7 %copy-start.2 = (s32[64]{0:T(128)S(1)}, s32[64]{0:T(128)}, u32[]{:S(2)}) copy-start(s32[64]{0:T(128)} %param.21) | copy-start | bytes 772
Sparse Core Ops, SparseCore 0:
  17.0 109.3 all-gather.1
where the time goes:
time: 208 us; the launch traced here: 207 us
  waiting for transfers between devices  98.4 us (47%)
  matrix products  42.4 us (20%)
  other arithmetic  20.1 us (10%)
  local copies, waits for them, and re-layouts  20.1 us (10%)
  between operations  15.5 us (7%)
  loops' own time  5.28 us (3%)
  starting transfers between devices  4.97 us (2%)
    all_gather x1, waiting for transfers between devices, side_by_side(): lax.all_gather(both, axis, axis=dim, tiled=True)  94.8 us
    dot_general x8, matrix products, attend(): jnp.einsum('hqd,khd->hqk', queries, key_rows, preferred_element_type=jnp....  20.4 us
    dot_general x8, matrix products, attend(): jnp.einsum('hqk,khd->hqd', weights.astype(jnp.bfloat16), value_rows, pref...  19.8 us
    reduce_sum x8, other arithmetic, attend(): totals = totals * shrink + jnp.sum(weights, axis=2)  10 us
    split x1, local copies, waits for them, and re-layouts, side_by_side(): jnp.split(lax.all_gather(both, axis, axis=dim, tiled=True), ends, axis=al...  8.86 us
    all_to_all x1, starting transfers between devices, sent_to_all(): lax.all_to_all(jnp.broadcast_to(value[None], (size, *value.shape)), axis,...  4.93 us
    another operation x1, loops' own time, absorb(): lax.scan(advance, running, (key_blocks, value_blocks, jnp.arange(block_co...  4.82 us
    dynamic_slice x8, local copies, waits for them, and re-layouts, absorb(): lax.scan(advance, running, (key_blocks, value_blocks, jnp.arange(block_co...  4.64 us
  transfers between devices with their start and end apart: 2, of which 2 were waited for; matrix products, arithmetic and copies ran while one was open for 3% of the time, Pallas kernels for 0%

commit v1 on v0

v1 whole, which is shorter than its diff:
```python
import functools
import math

import jax
import jax.numpy as jnp
from jax import lax
from jax.experimental import pallas as pl
from jax.experimental.pallas import tpu as pltpu
from jax.sharding import PartitionSpec as P

HEADS = 64
KV_HEADS = 8
HEAD_DIM = 128
HEADS_PER = HEADS // KV_HEADS
Z_HI, Y, CORES = 4, 8, 2
SLOTS = 48
GROUP_LEN = 320
ROWS = SLOTS * HEADS_PER
STAT_ROWS = 16
PAIR = CORES * GROUP_LEN
NEG_FILL = -1e30
EXP2_SCALE = math.log2(math.e) / math.sqrt(HEAD_DIM)
SCORE_SCALE = 1.0 / math.sqrt(HEAD_DIM)

VMEM = pl.BlockSpec(memory_space=pltpu.VMEM)
SMEM = pl.BlockSpec(memory_space=pltpu.SMEM)


def ctx_index(z_hi, y, core):
    return (z_hi * Y + y) * CORES + core


def mirrored(z_hi, y):
    return z_hi ^ ((Z_HI - 1) * (y & 1))


QUERY_GROUPS = [
    [ctx_index(mirrored(z, y), y, c) for y in range(Y)] for z in range(Z_HI) for c in range(CORES)
]
KEY_GROUPS = [[ctx_index(z, y, c) for z in range(Z_HI)] for y in range(Y) for c in range(CORES)]
CORE_SWAP = [(i, i ^ 1) for i in range(Z_HI * Y * CORES)]


def inverse_freq():
    half_dim = HEAD_DIM // 2
    exponent = jnp.arange(half_dim, dtype=jnp.float32) * 2.0 / HEAD_DIM
    base_freq = 1.0 / 500000.0**exponent
    wavelength = 2.0 * jnp.pi / base_freq
    smooth = (8192.0 / wavelength - 1.0) / 3.0
    blended_freq = (1.0 - smooth) * base_freq / 8.0 + smooth * base_freq
    return jnp.where(
        wavelength < 2048.0,
        base_freq,
        jnp.where(wavelength > 8192.0, base_freq / 8.0, blended_freq),
    )


def iota(shape, dim):
    return lax.broadcasted_iota(jnp.int32, shape, dim)


def column_of(row):
    n = row.shape[1]
    eye = iota((n, n), 0) == iota((n, n), 1)
    return jnp.sum(jnp.where(eye, jnp.broadcast_to(row, (n, n)), 0.0), axis=1, keepdims=True)


def row_of(wide):
    n = wide.shape[0]
    eye = iota((n, n), 0) == iota((n, n), 1)
    return jnp.sum(jnp.where(eye, wide, 0.0), axis=0, keepdims=True)


def prepare_kernel(
    offsets, count_ref, index_ref, freq_ref, q_ref, ck_ref, cv_ref, fk_ref, fv_ref,
    q_out, kv_out, jk_out, jv_out, drift_out,
):
    own_start = offsets[lax.axis_index("ctx")]
    count = count_ref[0]
    half = HEAD_DIM // 2
    index_row = index_ref[...]
    index_col = column_of(index_row.astype(jnp.float32))
    freq = freq_ref[...]
    start_row = jnp.full((1, HEAD_DIM), own_start, jnp.int32).astype(jnp.float32)
    slot_angle = (index_col + start_row[:, :1]) * freq
    group_angle = start_row * freq
    sign = jnp.where(iota((1, HEAD_DIM), 1) < half, -1.0, 1.0)
    slot_cos, slot_sin = jnp.cos(slot_angle), jnp.sin(slot_angle) * sign
    group_cos, group_sin = jnp.cos(group_angle), jnp.sin(group_angle) * sign

    def turn(rows, cosine, sine):
        x = rows.astype(jnp.float32)
        return (x * cosine + pltpu.roll(x, half, 1) * sine).astype(jnp.bfloat16)

    for h in range(HEADS_PER):
        head = turn(q_ref[:, h * HEAD_DIM : (h + 1) * HEAD_DIM], slot_cos, slot_sin)
        for y in range(Y):
            q_out[y, h * SLOTS : (h + 1) * SLOTS, :] = head

    turned = turn(ck_ref[...], group_cos, group_sin)
    fresh = turn(fk_ref[...], slot_cos, slot_sin)
    cached_values = cv_ref[...]
    fresh_values = fv_ref[...]

    live = iota((1, SLOTS), 1) < count
    chosen = jnp.where(live, index_row, -1)
    picker = jnp.where(iota((GROUP_LEN, SLOTS), 0) == chosen, 1.0, 0.0)
    covered = jnp.sum(picker, axis=1, keepdims=True) > 0.0
    picker = picker.astype(jnp.bfloat16)
    joined_keys = jnp.where(
        covered,
        jnp.dot(picker, fresh, preferred_element_type=jnp.float32),
        turned.astype(jnp.float32),
    ).astype(jnp.bfloat16)
    joined_values = jnp.where(
        covered,
        jnp.dot(picker, fresh_values, preferred_element_type=jnp.float32),
        cached_values.astype(jnp.float32),
    ).astype(jnp.bfloat16)
    jk_out[...] = joined_keys
    jv_out[...] = joined_values
    kv_out[:, :HEAD_DIM] = joined_keys
    kv_out[:, HEAD_DIM:] = joined_values

    reader = jnp.where(
        iota((SLOTS, GROUP_LEN), 1).astype(jnp.float32) == index_col, 1.0, 0.0
    ).astype(jnp.bfloat16)
    key_gap = fresh.astype(jnp.float32) - jnp.dot(
        reader, turned, preferred_element_type=jnp.float32
    )
    value_gap = fresh_values.astype(jnp.float32) - jnp.dot(
        reader, cached_values, preferred_element_type=jnp.float32
    )
    squares = jnp.sum(key_gap * key_gap + value_gap * value_gap, axis=1, keepdims=True)
    drift_row = row_of(jnp.broadcast_to(squares, (SLOTS, SLOTS)))
    for h in range(KV_HEADS):
        drift_out[h] = drift_row


def attend_kernel(index_ref, q_ref, own_ref, other_ref, out_ref, keys, values, scores, peaks):
    me = lax.axis_index("ctx")
    core = lax.rem(me, CORES)
    y_own = lax.rem(me // CORES, Y)
    z_own = me // (CORES * Y)
    z_group = jnp.where(lax.rem(y_own, 2) == 1, Z_HI - 1 - z_own, z_own)

    ones = jnp.ones((GROUP_LEN, HEAD_DIM), jnp.bfloat16)
    for z in range(Z_HI):
        for part, ref in enumerate((own_ref, other_ref)):
            source = slice(z * GROUP_LEN, (z + 1) * GROUP_LEN)
            target = slice(part * GROUP_LEN, (part + 1) * GROUP_LEN)
            keys[z, target, :] = ref[source, :HEAD_DIM]
            values[z, target, :HEAD_DIM] = ref[source, HEAD_DIM:]
            values[z, target, HEAD_DIM:] = ones

    def score(queries, block):
        return lax.dot_general(
            queries, keys[block], (((1,), (1,)), ((), ())), preferred_element_type=jnp.float32
        )

    def note(block, found):
        scores[block] = found
        top = found[:, :HEAD_DIM]
        for at in range(HEAD_DIM, PAIR, HEAD_DIM):
            top = jnp.maximum(top, found[:, at : at + HEAD_DIM])
        peaks[...] = jnp.maximum(peaks[...], top)

    def one_group(y, carry):
        z_query = jnp.where(lax.rem(y, 2) == 1, Z_HI - 1 - z_group, z_group)
        whole = z_query + jnp.where(y_own < y, 1, 0)
        queries = q_ref[y]
        peaks[...] = jnp.full((ROWS, HEAD_DIM), NEG_FILL, jnp.float32)

        def full(block, inner):
            note(block, score(queries, block))
            return inner

        lax.fori_loop(0, whole, full, 0)

        @pl.when(y == y_own)
        def _():
            found = score(queries, whole)
            index_col = column_of(index_ref[...].astype(jnp.float32))
            reach = jnp.concatenate([index_col] * HEADS_PER, axis=0)
            token = iota((1, PAIR), 1)
            place = jnp.where(
                token < GROUP_LEN, token, jnp.where(core == 1, -1, 2 * GROUP_LEN)
            ).astype(jnp.float32)
            note(whole, jnp.where(place <= reach, found, NEG_FILL))

        blocks = whole + jnp.where(y == y_own, 1, 0)
        peak = jnp.max(peaks[...], axis=1, keepdims=True)

        def weigh(block, total):
            weights = jnp.exp2((scores[block] - peak) * EXP2_SCALE).astype(jnp.bfloat16)
            return total + jnp.dot(weights, values[block], preferred_element_type=jnp.float32)

        total = lax.fori_loop(
            0, blocks, weigh, jnp.zeros((ROWS, 2 * HEAD_DIM), jnp.float32)
        )
        mass = total[:, HEAD_DIM:]
        seen = mass > 0.0
        safe = jnp.where(seen, mass, 1.0)
        out_ref[y, :ROWS, :] = (total[:, :HEAD_DIM] / safe).astype(jnp.bfloat16)
        level = jnp.where(seen, peak * SCORE_SCALE + jnp.log(safe), NEG_FILL)
        stat = jnp.zeros((STAT_ROWS, HEAD_DIM), jnp.float32)
        row = iota((STAT_ROWS, HEAD_DIM), 0)
        for k in range(ROWS // HEAD_DIM):
            rest = row_of(level[k * HEAD_DIM : (k + 1) * HEAD_DIM])
            for piece in range(3):
                part = rest.astype(jnp.bfloat16).astype(jnp.float32)
                stat = jnp.where(row == 3 * piece + k, part, stat)
                rest = rest - part
        out_ref[y, ROWS:, :] = stat.astype(jnp.bfloat16)
        return carry

    lax.fori_loop(0, Y, one_group, 0)


def merge_kernel(count_ref, parts_ref, out_ref):
    live = iota((SLOTS, HEAD_DIM), 0) < count_ref[0]
    eye = iota((HEAD_DIM, HEAD_DIM), 0) == iota((HEAD_DIM, HEAD_DIM), 1)
    stats = [parts_ref[y, ROWS:, :].astype(jnp.float32) for y in range(Y)]
    merged = []
    for k in range(ROWS // HEAD_DIM):
        levels = [s[k : k + 1] + s[k + 3 : k + 4] + s[k + 6 : k + 7] for s in stats]
        top = functools.reduce(jnp.maximum, levels)
        shares = [jnp.exp(level - top) for level in levels]
        whole = functools.reduce(jnp.add, shares)
        total = jnp.zeros((HEAD_DIM, HEAD_DIM), jnp.float32)
        for y in range(Y):
            share = jnp.broadcast_to(shares[y] / whole, (HEAD_DIM, HEAD_DIM))
            share = jnp.sum(jnp.where(eye, share, 0.0), axis=1, keepdims=True)
            part = parts_ref[y, k * HEAD_DIM : (k + 1) * HEAD_DIM, :].astype(jnp.float32)
            total = total + share * part
        merged.append(total)
    merged = jnp.concatenate(merged, axis=0)
    for h in range(HEADS_PER):
        head = jnp.where(live, merged[h * SLOTS : (h + 1) * SLOTS], 0.0)
        out_ref[:, h * HEAD_DIM : (h + 1) * HEAD_DIM] = head.astype(jnp.bfloat16)


def kernel_params(mib):
    return pltpu.CompilerParams(vmem_limit_bytes=mib << 20)


def shards(
    queries,
    cached_keys,
    cached_values,
    fresh_keys,
    fresh_values,
    recompute_index,
    recompute_count,
    group_offsets,
):
    bf16, f32 = jnp.bfloat16, jnp.float32
    shape = jax.ShapeDtypeStruct
    freq = inverse_freq()
    freq = jnp.concatenate([freq, freq])[None, :]
    copies, own_kv, joined_keys, joined_values, squares = pl.pallas_call(
        prepare_kernel,
        out_shape=(
            shape((Y, ROWS, HEAD_DIM), bf16),
            shape((GROUP_LEN, 2 * HEAD_DIM), bf16),
            shape((GROUP_LEN, HEAD_DIM), bf16),
            shape((GROUP_LEN, HEAD_DIM), bf16),
            shape((KV_HEADS, 1, SLOTS), f32),
        ),
        in_specs=[SMEM, SMEM] + [VMEM] * 7,
        out_specs=[VMEM] * 5,
        compiler_params=kernel_params(16),
        name="prepare",
    )(
        group_offsets, recompute_count, recompute_index, freq,
        queries, cached_keys, cached_values, fresh_keys, fresh_values,
    )

    all_queries = lax.all_to_all(
        copies, "ctx", 0, 0, axis_index_groups=QUERY_GROUPS, tiled=True
    )
    core_kv = lax.all_gather(own_kv, "ctx", axis=0, axis_index_groups=KEY_GROUPS, tiled=True)
    other_kv = lax.ppermute(core_kv, "ctx", CORE_SWAP)

    partial = pl.pallas_call(
        attend_kernel,
        out_shape=shape((Y, ROWS + STAT_ROWS, HEAD_DIM), bf16),
        in_specs=[VMEM] * 4,
        out_specs=VMEM,
        scratch_shapes=[
            pltpu.VMEM((Z_HI, PAIR, HEAD_DIM), bf16),
            pltpu.VMEM((Z_HI, PAIR, 2 * HEAD_DIM), bf16),
            pltpu.VMEM((Z_HI, ROWS, PAIR), f32),
            pltpu.VMEM((ROWS, HEAD_DIM), f32),
        ],
        compiler_params=kernel_params(28),
        name="attend",
    )(recompute_index, all_queries, core_kv, other_kv)

    squares, partial = lax.optimization_barrier((squares, partial))
    parts = lax.all_to_all(partial, "ctx", 0, 0, axis_index_groups=QUERY_GROUPS, tiled=True)
    drift = lax.all_to_all(squares, "head", 0, 0, tiled=True).sum(axis=0)
    drift = drift / (2.0 * KV_HEADS * HEAD_DIM)
    drift = jnp.where(iota((1, SLOTS), 1) < recompute_count[0], drift, 0.0)

    attention = pl.pallas_call(
        merge_kernel,
        out_shape=shape((SLOTS, HEADS_PER * HEAD_DIM), bf16),
        in_specs=[SMEM, VMEM],
        out_specs=VMEM,
        compiler_params=kernel_params(16),
        name="merge",
    )(recompute_count, parts)
    return (attention, joined_keys, joined_values, drift)


def solution(mesh):
    return jax.shard_map(
        shards,
        mesh=mesh,
        in_specs=(
            P("ctx", "head"),
            P("ctx", "head"),
            P("ctx", "head"),
            P("ctx", "head"),
            P("ctx", "head"),
            P("ctx", None),
            P("ctx"),
            P(),
        ),
        out_specs=(P("ctx", "head"), P("ctx", "head"), P("ctx", "head"), P("ctx", None)),
        check_vma=False,
    )
```

time: 208 us -> 119 us (0.57)
  the two profiles are of different devices: /device:TPU:441 before, /device:TPU:8 now
where the time goes in v1:
time: 119 us; the launch traced here: 118 us
  blocking collectives  43 us (36%)
  starting transfers between devices  26.3 us (22%)
  waiting for transfers between devices  23.2 us (19%)
  Pallas kernels  18.9 us (16%)
  local copies, waits for them, and re-layouts  4.66 us (4%)
  between operations  1.32 us (1%)
    all_gather x1, blocking collectives, shards(): lax.all_gather(own_kv, 'ctx', axis=0, axis_index_groups=KEY_GROUPS, tiled...  31.5 us
    all_to_all x1, waiting for transfers between devices, shards(): lax.all_to_all(partial, 'ctx', 0, 0, axis_index_groups=QUERY_GROUPS, tile...  21.1 us
    all_to_all x1, starting transfers between devices, shards(): lax.all_to_all(copies, 'ctx', 0, 0, axis_index_groups=QUERY_GROUPS, tiled...  16 us
    pallas_call x1, Pallas kernels, shards(): pl.pallas_call(attend_kernel, out_shape=shape((Y, ROWS + STAT_ROWS, HEAD_...  15.8 us
    all_to_all x1, blocking collectives, shards(): drift = lax.all_to_all(squares, 'head', 0, 0, tiled=True).sum(axis=0)  11.5 us
    all_to_all x1, starting transfers between devices, shards(): lax.all_to_all(partial, 'ctx', 0, 0, axis_index_groups=QUERY_GROUPS, tile...  8.42 us
    unnamed x14, local copies, waits for them, and re-layouts  4.66 us
  transfers between devices with their start and end apart: 3, of which 2 were waited for; matrix products, arithmetic and copies ran while one was open for 0% of the time, Pallas kernels for 0%

profile of v1, /device:TPU:8, one launch (start us, length us, event | category | flops | bytes accessed | tf_op | source)
XLA Modules:
  0.0 118.0 jit_solution(5240066339212875786)
XLA Ops:
  1.3 0.0 copy-start.5
  1.3 0.0 copy-start.6
  1.3 0.1 maximum_bitcast_fusion.freq_ref
  1.4 0.6 copy-done.5
  2.0 0.0 copy-done.6
  2.0 0.0 copy-start
  2.0 0.9 copy-done
  2.9 0.0 copy-start.1
  2.9 0.9 copy-done.1
  3.8 0.0 copy-start.2
  3.8 0.9 copy-done.2
  4.6 0.0 copy-start.3
  4.7 0.7 copy-done.3
  5.4 0.0 copy-start.4
  5.4 0.7 copy-done.4
  6.1 1.9 %prepare.1 = (bf16[8,384,128]{2,1,0:T(8,128)(2,1)}, bf16[320,256]{1,0:T(8,128)(2,1)S(1)}, bf16[320,128]{1,0:T(8,128)(2,1)}, bf16[320,128]{1,0:T(8,128)(2,1)}, f32[8,1,48]{2,1,0:T(1,128)S(1)}) custom-call(s32[64]{0:T(128)S(1)} %copy-done.6, s32[1]{0:T(128)} %copy.12.count_ref, s32[1,48]{1,0:T(1,128)S(1)} %copy-done.5, ...), custom_call_target="tpu_custom_call" | custom-call | tf_op jit(solution)/shard_map/prepare/pallas_call | solution.py:261
  8.0 16.0 %all-to-all-start = ((bf16[8,384,128]{2,1,0:T(8,128)(2,1)}), bf16[8,384,128]{2,1,0:T(8,128)(2,1)S(1)}, u32[]{:S(2)}, u32[]{:S(2)}) async-start(bf16[8,384,128]{2,1,0:T(8,128)(2,1)} %get-tuple-element.12), calls=%async_computation | async-start | bytes 1572864 | tf_op jit(solution)/shard_map/all_to_all | solution.py:279
  24.0 31.5 %all_gather.3.own_ref = bf16[1280,256]{1,0:T(8,128)(2,1)S(1)} all-gather(bf16[320,256]{1,0:T(8,128)(2,1)S(1)} %get-tuple-element.13), channel_id=1, replica_groups={{0,128,256,384},{8,136,264,392},{16,144,272,400},{24,152,280,408},{32,1..., dimensions={0}, use_global_device_ids=true | all-gather | bytes 819200 | tf_op jit(solution)/shard_map/all_gather | solution.py:282
  55.5 1.9 %collective-permute-start = (bf16[1280,256]{1,0:T(8,128)(2,1)S(1)}, bf16[1280,256]{1,0:T(8,128)(2,1)S(1)}, u32[]{:S(2)}, u32[]{:S(2)}) collective-permute-start(bf16[1280,256]{1,0:T(8,128)(2,1)S(1)} %all_gather.3.own_ref), channel_id=1, source_target_pairs={{0,8},{8,0},{16,24},{24,16},{32,40},{40,32},{48,56},{56,48},{64,72... | collective-permute-start | bytes 1966088 | tf_op jit(solution)/shard_map/ppermute | solution.py:283
  57.4 2.1 %collective-permute-done.other_ref = bf16[1280,256]{1,0:T(8,128)(2,1)S(1)} collective-permute-done((bf16[1280,256]{1,0:T(8,128)(2,1)S(1)}, bf16[1280,256]{1,0:T(8,128)(2,1)S(1)}, u32[]{:S(2)}, u32[]{:S(2)}) %collective-permute-start) | collective-permute-done | bytes 655392 | tf_op jit(solution)/shard_map/ppermute | solution.py:283
  59.4 0.0 all-to-all-done.q_ref
  59.4 15.8 %attend.1 = bf16[8,400,128]{2,1,0:T(8,128)(2,1)} custom-call(s32[1,48]{1,0:T(1,128)S(1)} %copy-done.5, bf16[8,384,128]{2,1,0:T(8,128)(2,1)S(1)} %all-to-all-done.q_ref, bf16[1280,256]{1,0:T(8,128)(2,1)S(1)} %all_gather.3.own_ref, bf16[1280,256]{1,0:T(8,128)(2,1)S(1)} %collective-permute-done.other_ref), custom_call_target="tpu_custom_call" | custom-call | tf_op jit(solution)/shard_map/attend/pallas_call | solution.py:285
  75.3 11.5 %all_to_all.15 = f32[8,1,48]{2,1,0:T(1,128)S(1)} all-to-all(f32[8,1,48]{2,1,0:T(1,128)S(1)} %get-tuple-element.17), channel_id=1, replica_groups=mesh['ctx'=64,'head'=8] {'head'}, dimensions={0} | all-to-all | bytes 3072 | tf_op jit(solution)/shard_map/all_to_all | solution.py:302
  86.8 8.4 %all-to-all-start.1 = ((bf16[8,400,128]{2,1,0:T(8,128)(2,1)}), bf16[8,400,128]{2,1,0:T(8,128)(2,1)S(1)}, u32[]{:S(2)}, u32[]{:S(2)}) async-start(bf16[8,400,128]{2,1,0:T(8,128)(2,1)} %attend.1), calls=%async_computation.1 | async-start | bytes 1638400 | tf_op jit(solution)/shard_map/all_to_all | solution.py:301
  95.3 0.5 compare_select_fusion
  95.8 21.1 %all-to-all-done.1.parts_ref = bf16[8,400,128]{2,1,0:T(8,128)(2,1)S(1)} async-done(((bf16[8,400,128]{2,1,0:T(8,128)(2,1)}), bf16[8,400,128]{2,1,0:T(8,128)(2,1)S(1)}, u32[]{:S(2)}, u32[]{:S(2)}) %all-to-all-start.1) | async-done | bytes 819232 | tf_op jit(solution)/shard_map/all_to_all | solution.py:301
  116.9 1.2 merge.1
  (2 shorter events, 0.0 us)
Async XLA Ops:
  1.3 0.7 copy-start.5
  1.3 0.7 copy-start.6
  2.0 0.9 copy-start
  2.9 0.9 copy-start.1
  3.8 0.9 copy-start.2
  4.6 0.7 copy-start.3
  5.4 0.7 copy-start.4
  8.0 51.5 %all-to-all-start = ((bf16[8,384,128]{2,1,0:T(8,128)(2,1)}), bf16[8,384,128]{2,1,0:T(8,128)(2,1)S(1)}, u32[]{:S(2)}, u32[]{:S(2)}) async-start(bf16[8,384,128]{2,1,0:T(8,128)(2,1)} %get-tuple-element.12), calls=%async_computation | async-start | bytes 1572864 | tf_op jit(solution)/shard_map/all_to_all | solution.py:279
  55.5 4.0 %collective-permute-start = (bf16[1280,256]{1,0:T(8,128)(2,1)S(1)}, bf16[1280,256]{1,0:T(8,128)(2,1)S(1)}, u32[]{:S(2)}, u32[]{:S(2)}) collective-permute-start(bf16[1280,256]{1,0:T(8,128)(2,1)S(1)} %all_gather.3.own_ref), channel_id=1, source_target_pairs={{0,8},{8,0},{16,24},{24,16},{32,40},{40,32},{48,56},{56,48},{64,72... | collective-permute-start | bytes 1966088 | tf_op jit(solution)/shard_map/ppermute | solution.py:283
  86.8 30.1 %all-to-all-start.1 = ((bf16[8,400,128]{2,1,0:T(8,128)(2,1)}), bf16[8,400,128]{2,1,0:T(8,128)(2,1)S(1)}, u32[]{:S(2)}, u32[]{:S(2)}) async-start(bf16[8,400,128]{2,1,0:T(8,128)(2,1)} %attend.1), calls=%async_computation.1 | async-start | bytes 1638400 | tf_op jit(solution)/shard_map/all_to_all | solution.py:301

commit v2 on v1

--- a/solution.py
+++ b/solution.py
@@ -7,6 +7,7 @@
 from jax.experimental import pallas as pl
 from jax.experimental.pallas import tpu as pltpu
 from jax.sharding import PartitionSpec as P
+
 
 HEADS = 64
 KV_HEADS = 8
@@ -24,19 +25,14 @@
 
 VMEM = pl.BlockSpec(memory_space=pltpu.VMEM)
 SMEM = pl.BlockSpec(memory_space=pltpu.SMEM)
+HBM = pl.BlockSpec(memory_space=pltpu.HBM)
 
 
 def ctx_index(z_hi, y, core):
     return (z_hi * Y + y) * CORES + core
 
 
-def mirrored(z_hi, y):
-    return z_hi ^ ((Z_HI - 1) * (y & 1))
-
-
-QUERY_GROUPS = [
-    [ctx_index(mirrored(z, y), y, c) for y in range(Y)] for z in range(Z_HI) for c in range(CORES)
-]
+QUERY_GROUPS = [[ctx_index(z, y, c) for y in range(Y)] for z in range(Z_HI) for c in range(CORES)]
 KEY_GROUPS = [[ctx_index(z, y, c) for z in range(Z_HI)] for y in range(Y) for c in range(CORES)]
 CORE_SWAP = [(i, i ^ 1) for i in range(Z_HI * Y * CORES)]
 
@@ -72,9 +68,20 @@
 
 
 def prepare_kernel(
-    offsets, count_ref, index_ref, freq_ref, q_ref, ck_ref, cv_ref, fk_ref, fv_ref,
+    offsets, count_ref, freq_ref, index_hbm, q_hbm, ck_hbm, cv_hbm, fk_hbm, fv_hbm,
     q_out, kv_out, jk_out, jv_out, drift_out,
+    index_ref, q_ref, ck_ref, cv_ref, fk_ref, fv_ref, arrived,
 ):
+    copies = [
+        pltpu.make_async_copy(source, target, arrived.at[i])
+        for i, (source, target) in enumerate((
+            (index_hbm, index_ref), (q_hbm, q_ref), (fk_hbm, fk_ref),
+            (ck_hbm, ck_ref), (fv_hbm, fv_ref), (cv_hbm, cv_ref),
+        ))
+    ]
+    for copy in copies:
+        copy.start()
+    copies[0].wait()
     own_start = offsets[lax.axis_index("ctx")]
     count = count_ref[0]
     half = HEAD_DIM // 2
@@ -92,6 +99,8 @@
         x = rows.astype(jnp.float32)
         return (x * cosine + pltpu.roll(x, half, 1) * sine).astype(jnp.bfloat16)
 
+    for copy in copies[1:]:
+        copy.wait()
     for h in range(HEADS_PER):
         head = turn(q_ref[:, h * HEAD_DIM : (h + 1) * HEAD_DIM], slot_cos, slot_sin)
         for y in range(Y):
@@ -133,76 +142,75 @@
     )
     squares = jnp.sum(key_gap * key_gap + value_gap * value_gap, axis=1, keepdims=True)
     drift_row = row_of(jnp.broadcast_to(squares, (SLOTS, SLOTS)))
-    for h in range(KV_HEADS):
-        drift_out[h] = drift_row
-
-
-def attend_kernel(index_ref, q_ref, own_ref, other_ref, out_ref, keys, values, scores, peaks):
+    drift_out[...] = drift_row
+
+
+def attend_kernel(
+    index_ref, q_ref, own_ref, other_ref, out_ref, keys, values, reach_ref,
+    scores_even, scores_odd, peaks_even, peaks_odd,
+):
     me = lax.axis_index("ctx")
     core = lax.rem(me, CORES)
     y_own = lax.rem(me // CORES, Y)
     z_own = me // (CORES * Y)
-    z_group = jnp.where(lax.rem(y_own, 2) == 1, Z_HI - 1 - z_own, z_own)
 
     ones = jnp.ones((GROUP_LEN, HEAD_DIM), jnp.bfloat16)
     for z in range(Z_HI):
         for part, ref in enumerate((own_ref, other_ref)):
             source = slice(z * GROUP_LEN, (z + 1) * GROUP_LEN)
-            target = slice(part * GROUP_LEN, (part + 1) * GROUP_LEN)
-            keys[z, target, :] = ref[source, :HEAD_DIM]
-            values[z, target, :HEAD_DIM] = ref[source, HEAD_DIM:]
-            values[z, target, HEAD_DIM:] = ones
-
-    def score(queries, block):
-        return lax.dot_general(
-            queries, keys[block], (((1,), (1,)), ((), ())), preferred_element_type=jnp.float32
+            target = slice(z * PAIR + part * GROUP_LEN, z * PAIR + (part + 1) * GROUP_LEN)
+            keys[target, :] = ref[source, :HEAD_DIM]
+            values[target, :HEAD_DIM] = ref[source, HEAD_DIM:]
+            values[target, HEAD_DIM:] = ones
+
+    token = iota((1, PAIR), 1)
+    place = jnp.where(
+        token < GROUP_LEN, token, jnp.where(core == 1, -1, GROUP_LEN)
+    ).astype(jnp.float32)
+    index_col = column_of(index_ref[...].astype(jnp.float32))
+    reach_ref[...] = jnp.broadcast_to(
+        jnp.concatenate([index_col] * HEADS_PER, axis=0), (ROWS, HEAD_DIM)
+    )
+
+    def score(y, blocks, masked, scores, peaks):
+        queries = q_ref[y]
+        reach = jnp.where(
+            y == y_own, reach_ref[...], jnp.where(y_own < y, 2.0 * GROUP_LEN, -2.0)
         )
-
-    def note(block, found):
-        scores[block] = found
-        top = found[:, :HEAD_DIM]
-        for at in range(HEAD_DIM, PAIR, HEAD_DIM):
-            top = jnp.maximum(top, found[:, at : at + HEAD_DIM])
-        peaks[...] = jnp.maximum(peaks[...], top)
-
-    def one_group(y, carry):
-        z_query = jnp.where(lax.rem(y, 2) == 1, Z_HI - 1 - z_group, z_group)
-        whole = z_query + jnp.where(y_own < y, 1, 0)
-        queries = q_ref[y]
-        peaks[...] = jnp.full((ROWS, HEAD_DIM), NEG_FILL, jnp.float32)
-
-        def full(block, inner):
-            note(block, score(queries, block))
-            return inner
-
-        lax.fori_loop(0, whole, full, 0)
-
-        @pl.when(y == y_own)
-        def _():
-            found = score(queries, whole)
-            index_col = column_of(index_ref[...].astype(jnp.float32))
-            reach = jnp.concatenate([index_col] * HEADS_PER, axis=0)
-            token = iota((1, PAIR), 1)
-            place = jnp.where(
-                token < GROUP_LEN, token, jnp.where(core == 1, -1, 2 * GROUP_LEN)
-            ).astype(jnp.float32)
-            note(whole, jnp.where(place <= reach, found, NEG_FILL))
-
-        blocks = whole + jnp.where(y == y_own, 1, 0)
-        peak = jnp.max(peaks[...], axis=1, keepdims=True)
-
-        def weigh(block, total):
-            weights = jnp.exp2((scores[block] - peak) * EXP2_SCALE).astype(jnp.bfloat16)
-            return total + jnp.dot(weights, values[block], preferred_element_type=jnp.float32)
-
-        total = lax.fori_loop(
-            0, blocks, weigh, jnp.zeros((ROWS, 2 * HEAD_DIM), jnp.float32)
+        top = None
+        for block in range(blocks):
+            found = lax.dot_general(
+                queries,
+                keys[block * PAIR : (block + 1) * PAIR, :],
+                (((1,), (1,)), ((), ())),
+                preferred_element_type=jnp.float32,
+            )
+            limit = None
+            if block in masked:
+                limit = jnp.where(
+                    z_own == block, reach, jnp.where(block < z_own, 2.0 * GROUP_LEN, -2.0)
+                )
+            for at in range(0, PAIR, HEAD_DIM):
+                part = found[:, at : at + HEAD_DIM]
+                if limit is not None:
+                    part = jnp.where(place[:, at : at + HEAD_DIM] <= limit, part, NEG_FILL)
+                scores[:, block * PAIR + at : block * PAIR + at + HEAD_DIM] = part
+                top = part if top is None else jnp.maximum(top, part)
+        peaks[...] = jnp.broadcast_to(jnp.max(top, axis=1, keepdims=True), (ROWS, HEAD_DIM))
+
+    def weigh(y, blocks, scores, peaks):
+        peak = peaks[...]
+        size = blocks * PAIR
+        weights = [
+            jnp.exp2((scores[:, at : at + HEAD_DIM] - peak) * EXP2_SCALE).astype(jnp.bfloat16)
+            for at in range(0, size, HEAD_DIM)
+        ]
+        total = jnp.dot(
+            jnp.concatenate(weights, axis=1), values[:size, :], preferred_element_type=jnp.float32
         )
         mass = total[:, HEAD_DIM:]
-        seen = mass > 0.0
-        safe = jnp.where(seen, mass, 1.0)
-        out_ref[y, :ROWS, :] = (total[:, :HEAD_DIM] / safe).astype(jnp.bfloat16)
-        level = jnp.where(seen, peak * SCORE_SCALE + jnp.log(safe), NEG_FILL)
+        out_ref[y, :ROWS, :] = (total[:, :HEAD_DIM] / mass).astype(jnp.bfloat16)
+        level = jnp.where(peak > 0.5 * NEG_FILL, peak * SCORE_SCALE + jnp.log(mass), NEG_FILL)
         stat = jnp.zeros((STAT_ROWS, HEAD_DIM), jnp.float32)
         row = iota((STAT_ROWS, HEAD_DIM), 0)
         for k in range(ROWS // HEAD_DIM):
@@ -212,9 +220,28 @@
                 stat = jnp.where(row == 3 * piece + k, part, stat)
                 rest = rest - part
         out_ref[y, ROWS:, :] = stat.astype(jnp.bfloat16)
-        return carry
-
-    lax.fori_loop(0, Y, one_group, 0)
+
+    def all_groups(blocks, masked):
+        even, odd = (scores_even, peaks_even), (scores_odd, peaks_odd)
+        score(0, blocks, masked, *even)
+
+        def step(pair, carry):
+            y = 2 * pair
+            score(y + 1, blocks, masked, *odd)
+            weigh(y, blocks, *even)
+            score(jnp.minimum(y + 2, Y - 1), blocks, masked, *even)
+            weigh(y + 1, blocks, *odd)
+            return carry
+
+        lax.fori_loop(0, Y // 2, step, 0)
+
+    @pl.when(z_own == Z_HI - 1)
+    def _():
+        all_groups(Z_HI, (Z_HI - 1,))
+
+    @pl.when(z_own != Z_HI - 1)
+    def _():
+        all_groups(Z_HI - 1, tuple(range(Z_HI - 1)))
 
 
 def merge_kernel(count_ref, parts_ref, out_ref):
@@ -265,14 +292,22 @@
             shape((GROUP_LEN, 2 * HEAD_DIM), bf16),
             shape((GROUP_LEN, HEAD_DIM), bf16),
             shape((GROUP_LEN, HEAD_DIM), bf16),
-            shape((KV_HEADS, 1, SLOTS), f32),
+            shape((1, SLOTS), f32),
         ),
-        in_specs=[SMEM, SMEM] + [VMEM] * 7,
+        in_specs=[SMEM, SMEM, VMEM] + [HBM] * 6,
         out_specs=[VMEM] * 5,
-        compiler_params=kernel_params(16),
+        scratch_shapes=[
+            pltpu.VMEM((1, SLOTS), jnp.int32),
+            pltpu.VMEM((SLOTS, HEADS_PER * HEAD_DIM), bf16),
+            pltpu.VMEM((GROUP_LEN, HEAD_DIM), bf16),
+            pltpu.VMEM((GROUP_LEN, HEAD_DIM), bf16),
+            pltpu.VMEM((SLOTS, HEAD_DIM), bf16),
+            pltpu.VMEM((SLOTS, HEAD_DIM), bf16),
+            pltpu.SemaphoreType.DMA((6,)),
+        ],
         name="prepare",
     )(
-        group_offsets, recompute_count, recompute_index, freq,
+        group_offsets, recompute_count, freq, recompute_index,
         queries, cached_keys, cached_values, fresh_keys, fresh_values,
     )
 
@@ -288,18 +323,23 @@
         in_specs=[VMEM] * 4,
         out_specs=VMEM,
         scratch_shapes=[
-            pltpu.VMEM((Z_HI, PAIR, HEAD_DIM), bf16),
-            pltpu.VMEM((Z_HI, PAIR, 2 * HEAD_DIM), bf16),
-            pltpu.VMEM((Z_HI, ROWS, PAIR), f32),
+            pltpu.VMEM((Z_HI * PAIR, HEAD_DIM), bf16),
+            pltpu.VMEM((Z_HI * PAIR, 2 * HEAD_DIM), bf16),
+            pltpu.VMEM((ROWS, HEAD_DIM), f32),
+            pltpu.VMEM((ROWS, Z_HI * PAIR), f32),
+            pltpu.VMEM((ROWS, Z_HI * PAIR), f32),
+            pltpu.VMEM((ROWS, HEAD_DIM), f32),
             pltpu.VMEM((ROWS, HEAD_DIM), f32),
         ],
         compiler_params=kernel_params(28),
         name="attend",
     )(recompute_index, all_queries, core_kv, other_kv)
 
-    squares, partial = lax.optimization_barrier((squares, partial))
-    parts = lax.all_to_all(partial, "ctx", 0, 0, axis_index_groups=QUERY_GROUPS, tiled=True)
-    drift = lax.all_to_all(squares, "head", 0, 0, tiled=True).sum(axis=0)
+    parts = lax.all_to_all(
+        partial, "ctx", 0, 0, axis_index_groups=QUERY_GROUPS, tiled=True
+    )
+    squares = lax.all_gather(squares, "head", axis=0, tiled=True)
+    drift = squares.sum(axis=0, keepdims=True)
     drift = drift / (2.0 * KV_HEADS * HEAD_DIM)
     drift = jnp.where(iota((1, SLOTS), 1) < recompute_count[0], drift, 0.0)
 

time: 119 us -> 83.7 us (0.70)
  the two profiles are of different devices: /device:TPU:8 before, /device:TPU:1 now
where the time goes in v2:
time: 83.7 us; the launch traced here: 83.3 us
  blocking collectives  37.2 us (44%)
  starting transfers between devices  19.1 us (23%)
  Pallas kernels  15 us (18%)
  waiting for transfers between devices  8.95 us (11%)
  between operations  1.33 us (2%)
  other arithmetic  1.15 us (1%)
    all_gather x1, blocking collectives, shards(): lax.all_gather(own_kv, 'ctx', axis=0, axis_index_groups=KEY_GROUPS, tiled...  21.4 us
    all_gather x1, blocking collectives, shards(): squares = lax.all_gather(squares, 'head', axis=0, tiled=True)  15.8 us
    pallas_call x1, Pallas kernels, shards(): pl.pallas_call(attend_kernel, out_shape=shape((Y, ROWS + STAT_ROWS, HEAD_...  10.9 us
    all_to_all x1, starting transfers between devices, shards(): lax.all_to_all(copies, 'ctx', 0, 0, axis_index_groups=QUERY_GROUPS, tiled...  7.78 us
    all_to_all x1, starting transfers between devices, shards(): lax.all_to_all(partial, 'ctx', 0, 0, axis_index_groups=QUERY_GROUPS, tile...  7.38 us
    all_to_all x1, waiting for transfers between devices, shards(): lax.all_to_all(partial, 'ctx', 0, 0, axis_index_groups=QUERY_GROUPS, tile...  7.24 us
    ppermute x1, starting transfers between devices, shards(): other_kv = lax.ppermute(core_kv, 'ctx', CORE_SWAP)  3.89 us
    pallas_call x1, Pallas kernels, shards(): pl.pallas_call(prepare_kernel, out_shape=(shape((Y, ROWS, HEAD_DIM), bf16...  2.88 us
  transfers between devices with their start and end apart: 3, of which 2 were waited for; matrix products, arithmetic and copies ran while one was open for 1% of the time, Pallas kernels for 0%

profile of v2, /device:TPU:1, one launch (start us, length us, event | category | flops | bytes accessed | tf_op | source)
XLA Modules:
  0.0 83.3 jit_solution(5009519268614946954)
XLA Ops:
  1.3 0.6 maximum_bitcast_fusion.freq_ref
  1.9 2.9 %prepare.1 = (bf16[8,384,128]{2,1,0:T(8,128)(2,1)}, bf16[320,256]{1,0:T(8,128)(2,1)}, bf16[320,128]{1,0:T(8,128)(2,1)}, bf16[320,128]{1,0:T(8,128)(2,1)}, f32[1,48]{1,0:T(1,128)}) custom-call(s32[64]{0:T(128)} %offsets.1, s32[1]{0:T(128)} %copy.12.count_ref, f32[1,128]{1,0:T(1,128)} %maximum_bitcast_fusion.freq_ref, s32[1,48]{1,0:T(1,128)} %index_ref.1, ...), custom_call_target="tpu_custom_call" | custom-call | tf_op jit(solution)/shard_map/prepare/pallas_call | solution.py:288
  4.8 0.0 copy-start.1
  4.8 7.8 %all-to-all-start = ((bf16[8,384,128]{2,1,0:T(8,128)(2,1)}), bf16[8,384,128]{2,1,0:T(8,128)(2,1)S(1)}, u32[]{:S(2)}, u32[]{:S(2)}) async-start(bf16[8,384,128]{2,1,0:T(8,128)(2,1)} %get-tuple-element.9), calls=%async_computation | async-start | bytes 1572864 | tf_op jit(solution)/shard_map/all_to_all | solution.py:314
  12.6 0.0 copy-done.1
  12.6 0.0 copy-start
  12.6 21.4 %all_gather.6.own_ref = bf16[1280,256]{1,0:T(8,128)(2,1)S(1)} all-gather(bf16[320,256]{1,0:T(8,128)(2,1)S(1)} %copy-done.1), channel_id=1, replica_groups={{0,128,256,384},{8,136,264,392},{16,144,272,400},{24,152,280,408},{32,1..., dimensions={0}, use_global_device_ids=true | all-gather | bytes 819200 | tf_op jit(solution)/shard_map/all_gather | solution.py:317
  33.9 3.9 %collective-permute-start = (bf16[1280,256]{1,0:T(8,128)(2,1)S(1)}, bf16[1280,256]{1,0:T(8,128)(2,1)S(1)}, u32[]{:S(2)}, u32[]{:S(2)}) collective-permute-start(bf16[1280,256]{1,0:T(8,128)(2,1)S(1)} %all_gather.6.own_ref), channel_id=1, source_target_pairs={{0,8},{8,0},{16,24},{24,16},{32,40},{40,32},{48,56},{56,48},{64,72... | collective-permute-start | bytes 1966088 | tf_op jit(solution)/shard_map/ppermute | solution.py:318
  37.8 1.7 %collective-permute-done.other_ref = bf16[1280,256]{1,0:T(8,128)(2,1)S(1)} collective-permute-done((bf16[1280,256]{1,0:T(8,128)(2,1)S(1)}, bf16[1280,256]{1,0:T(8,128)(2,1)S(1)}, u32[]{:S(2)}, u32[]{:S(2)}) %collective-permute-start) | collective-permute-done | bytes 655392 | tf_op jit(solution)/shard_map/ppermute | solution.py:318
  39.5 0.0 all-to-all-done.q_ref
  39.6 0.0 copy-done
  39.6 10.9 %attend.1 = bf16[8,400,128]{2,1,0:T(8,128)(2,1)} custom-call(s32[1,48]{1,0:T(1,128)S(1)} %copy-done, bf16[8,384,128]{2,1,0:T(8,128)(2,1)S(1)} %all-to-all-done.q_ref, bf16[1280,256]{1,0:T(8,128)(2,1)S(1)} %all_gather.6.own_ref, bf16[1280,256]{1,0:T(8,128)(2,1)S(1)} %collective-permute-done.other_ref), custom_call_target="tpu_custom_call" | custom-call | tf_op jit(solution)/shard_map/attend/pallas_call | solution.py:320
  50.5 7.4 %all-to-all-start.1 = ((bf16[8,400,128]{2,1,0:T(8,128)(2,1)}), bf16[8,400,128]{2,1,0:T(8,128)(2,1)S(1)}, u32[]{:S(2)}, u32[]{:S(2)}) async-start(bf16[8,400,128]{2,1,0:T(8,128)(2,1)} %attend.1), calls=%async_computation.1 | async-start | bytes 1638400 | tf_op jit(solution)/shard_map/all_to_all | solution.py:338
  57.9 0.0 copy-start.2
  57.9 0.7 copy-done.2
  58.5 15.8 %all-gather = f32[8,1,48]{2,1,0:T(1,128)S(1)} all-gather(f32[1,1,48]{2,1,0:T(1,128)S(1)} %bitcast.7), channel_id=1, replica_groups=mesh['ctx'=64,'head'=8] {'head'}, dimensions={0}, use_global_device_ids=true | all-gather | bytes 1728 | tf_op jit(solution)/shard_map/all_gather | solution.py:341
  74.4 0.5 compare_select_fusion
  74.9 7.2 %all-to-all-done.1.parts_ref = bf16[8,400,128]{2,1,0:T(8,128)(2,1)S(1)} async-done(((bf16[8,400,128]{2,1,0:T(8,128)(2,1)}), bf16[8,400,128]{2,1,0:T(8,128)(2,1)S(1)}, u32[]{:S(2)}, u32[]{:S(2)}) %all-to-all-start.1) | async-done | bytes 819232 | tf_op jit(solution)/shard_map/all_to_all | solution.py:338
  82.2 1.2 %merge.1 = bf16[48,1024]{1,0:T(8,128)(2,1)} custom-call(s32[1]{0:T(128)} %copy.12.count_ref, bf16[8,400,128]{2,1,0:T(8,128)(2,1)S(1)} %all-to-all-done.1.parts_ref), custom_call_target="tpu_custom_call" | custom-call | tf_op jit(solution)/shard_map/merge/pallas_call | solution.py:346
  (2 shorter events, 0.0 us)
Async XLA Ops:
  4.8 7.8 %copy-start.1 = (bf16[320,256]{1,0:T(8,128)(2,1)S(1)}, bf16[320,256]{1,0:T(8,128)(2,1)}, u32[]{:S(2)}) copy-start(bf16[320,256]{1,0:T(8,128)(2,1)} %get-tuple-element.10) | copy-start | bytes 491524
  4.8 34.8 %all-to-all-start = ((bf16[8,384,128]{2,1,0:T(8,128)(2,1)}), bf16[8,384,128]{2,1,0:T(8,128)(2,1)S(1)}, u32[]{:S(2)}, u32[]{:S(2)}) async-start(bf16[8,384,128]{2,1,0:T(8,128)(2,1)} %get-tuple-element.9), calls=%async_computation | async-start | bytes 1572864 | tf_op jit(solution)/shard_map/all_to_all | solution.py:314
  12.6 27.0 %copy-start = (s32[1,48]{1,0:T(1,128)S(1)}, s32[1,48]{1,0:T(1,128)}, u32[]{:S(2)}) copy-start(s32[1,48]{1,0:T(1,128)} %index_ref.1) | copy-start | bytes 580
  33.9 5.6 %collective-permute-start = (bf16[1280,256]{1,0:T(8,128)(2,1)S(1)}, bf16[1280,256]{1,0:T(8,128)(2,1)S(1)}, u32[]{:S(2)}, u32[]{:S(2)}) collective-permute-start(bf16[1280,256]{1,0:T(8,128)(2,1)S(1)} %all_gather.6.own_ref), channel_id=1, source_target_pairs={{0,8},{8,0},{16,24},{24,16},{32,40},{40,32},{48,56},{56,48},{64,72... | collective-permute-start | bytes 1966088 | tf_op jit(solution)/shard_map/ppermute | solution.py:318
  50.5 31.7 %all-to-all-start.1 = ((bf16[8,400,128]{2,1,0:T(8,128)(2,1)}), bf16[8,400,128]{2,1,0:T(8,128)(2,1)S(1)}, u32[]{:S(2)}, u32[]{:S(2)}) async-start(bf16[8,400,128]{2,1,0:T(8,128)(2,1)} %attend.1), calls=%async_computation.1 | async-start | bytes 1638400 | tf_op jit(solution)/shard_map/all_to_all | solution.py:338
  57.9 0.7 copy-start.2

commit v3 on v2

--- a/solution.py
+++ b/solution.py
@@ -17,8 +17,12 @@
 SLOTS = 48
 GROUP_LEN = 320
 ROWS = SLOTS * HEADS_PER
-STAT_ROWS = 16
-PAIR = CORES * GROUP_LEN
+STAT_ROWS = 8
+ONES = 16
+STEP = 256
+CHUNK = 256
+WIDE = 64
+SHORT = 1024
 NEG_FILL = -1e30
 EXP2_SCALE = math.log2(math.e) / math.sqrt(HEAD_DIM)
 SCORE_SCALE = 1.0 / math.sqrt(HEAD_DIM)
@@ -70,7 +74,7 @@
 def prepare_kernel(
     offsets, count_ref, freq_ref, index_hbm, q_hbm, ck_hbm, cv_hbm, fk_hbm, fv_hbm,
     q_out, kv_out, jk_out, jv_out, drift_out,
-    index_ref, q_ref, ck_ref, cv_ref, fk_ref, fv_ref, arrived,
+    index_ref, q_ref, ck_ref, cv_ref, fk_ref, fv_ref, turned_q, arrived, left,
 ):
     copies = [
         pltpu.make_async_copy(source, target, arrived.at[i])
@@ -99,13 +103,16 @@
         x = rows.astype(jnp.float32)
         return (x * cosine + pltpu.roll(x, half, 1) * sine).astype(jnp.bfloat16)
 
-    for copy in copies[1:]:
-        copy.wait()
+    copies[1].wait()
     for h in range(HEADS_PER):
         head = turn(q_ref[:, h * HEAD_DIM : (h + 1) * HEAD_DIM], slot_cos, slot_sin)
-        for y in range(Y):
-            q_out[y, h * SLOTS : (h + 1) * SLOTS, :] = head
-
+        turned_q[h * SLOTS : (h + 1) * SLOTS, :] = head
+    sends = [pltpu.make_async_copy(turned_q, q_out.at[y], left.at[y]) for y in range(Y)]
+    for send in sends:
+        send.start()
+
+    for copy in copies[2:]:
+        copy.wait()
     turned = turn(ck_ref[...], group_cos, group_sin)
     fresh = turn(fk_ref[...], slot_cos, slot_sin)
     cached_values = cv_ref[...]
@@ -143,128 +150,144 @@
     squares = jnp.sum(key_gap * key_gap + value_gap * value_gap, axis=1, keepdims=True)
     drift_row = row_of(jnp.broadcast_to(squares, (SLOTS, SLOTS)))
     drift_out[...] = drift_row
+    for send in sends:
+        send.wait()
 
 
 def attend_kernel(
-    index_ref, q_ref, own_ref, other_ref, out_ref, keys, values, reach_ref,
+    index_ref, q_ref, own_ref, other_ref, out_ref, values, own_limit, other_limit,
     scores_even, scores_odd, peaks_even, peaks_odd,
 ):
     me = lax.axis_index("ctx")
     core = lax.rem(me, CORES)
     y_own = lax.rem(me // CORES, Y)
     z_own = me // (CORES * Y)
-
-    ones = jnp.ones((GROUP_LEN, HEAD_DIM), jnp.bfloat16)
-    for z in range(Z_HI):
-        for part, ref in enumerate((own_ref, other_ref)):
-            source = slice(z * GROUP_LEN, (z + 1) * GROUP_LEN)
-            target = slice(z * PAIR + part * GROUP_LEN, z * PAIR + (part + 1) * GROUP_LEN)
-            keys[target, :] = ref[source, :HEAD_DIM]
-            values[target, :HEAD_DIM] = ref[source, HEAD_DIM:]
-            values[target, HEAD_DIM:] = ones
-
-    token = iota((1, PAIR), 1)
-    place = jnp.where(
-        token < GROUP_LEN, token, jnp.where(core == 1, -1, GROUP_LEN)
-    ).astype(jnp.float32)
+    gathered = Z_HI * GROUP_LEN
+    sources = (own_ref, own_limit), (other_ref, other_limit)
+
     index_col = column_of(index_ref[...].astype(jnp.float32))
-    reach_ref[...] = jnp.broadcast_to(
-        jnp.concatenate([index_col] * HEADS_PER, axis=0), (ROWS, HEAD_DIM)
-    )
-
-    def score(y, blocks, masked, scores, peaks):
-        queries = q_ref[y]
-        reach = jnp.where(
-            y == y_own, reach_ref[...], jnp.where(y_own < y, 2.0 * GROUP_LEN, -2.0)
+    slot = lax.rem(iota((SLOTS, ROWS), 1), SLOTS)
+    own_index = jnp.sum(
+        jnp.where(slot == iota((SLOTS, ROWS), 0), index_col, 0.0), axis=0, keepdims=True
+    )
+    before = z_own * GROUP_LEN - 1
+    full = before + GROUP_LEN
+    for y in range(Y):
+        lanes = slice(y * ROWS, (y + 1) * ROWS)
+        beside = jnp.where(y_own < y, full, before)
+        own_limit[:, lanes] = jnp.where(
+            y == y_own, own_index.astype(jnp.int32) + (before + 1), beside
         )
+        other_limit[:, lanes] = jnp.full(
+            (1, ROWS), jnp.where(jnp.logical_and(y == y_own, core == 1), full, beside), jnp.int32
+        )
+
+    def score(step, size, masked, scores, peaks):
+        lanes = pl.ds(pl.multiple_of(step * STEP, STEP), STEP)
+        queries = q_ref[lanes, :]
         top = None
-        for block in range(blocks):
-            found = lax.dot_general(
-                queries,
-                keys[block * PAIR : (block + 1) * PAIR, :],
-                (((1,), (1,)), ((), ())),
+        for part, (source, limit_ref) in enumerate(sources):
+            limit = limit_ref[:, lanes]
+            for at in range(0, size, CHUNK):
+                found = lax.dot_general(
+                    source[at : at + CHUNK, :HEAD_DIM],
+                    queries,
+                    (((1,), (1,)), ((), ())),
+                    preferred_element_type=jnp.float32,
+                )
+                if at + CHUNK > masked:
+                    found = jnp.where(iota((CHUNK, STEP), 0) <= limit - at, found, NEG_FILL)
+                scores[part * size + at : part * size + at + CHUNK, :] = found
+                for row in range(0, CHUNK, WIDE):
+                    tile = found[row : row + WIDE]
+                    top = tile if top is None else jnp.maximum(top, tile)
+        peaks[...] = jnp.max(top, axis=0, keepdims=True)
+
+    def weigh(step, size, scores, peaks):
+        peak = peaks[...]
+        total = jnp.zeros((HEAD_DIM + ONES, STEP), jnp.float32)
+        for part in range(2):
+            weights = []
+            for at in range(part * size, (part + 1) * size, CHUNK):
+                weight = jnp.exp2((scores[at : at + CHUNK, :] - peak) * EXP2_SCALE)
+                weights.append(weight.astype(jnp.bfloat16))
+            total = total + jnp.dot(
+                values[:, part * gathered : part * gathered + size],
+                jnp.concatenate(weights, axis=0),
                 preferred_element_type=jnp.float32,
             )
-            limit = None
-            if block in masked:
-                limit = jnp.where(
-                    z_own == block, reach, jnp.where(block < z_own, 2.0 * GROUP_LEN, -2.0)
-                )
-            for at in range(0, PAIR, HEAD_DIM):
-                part = found[:, at : at + HEAD_DIM]
-                if limit is not None:
-                    part = jnp.where(place[:, at : at + HEAD_DIM] <= limit, part, NEG_FILL)
-                scores[:, block * PAIR + at : block * PAIR + at + HEAD_DIM] = part
-                top = part if top is None else jnp.maximum(top, part)
-        peaks[...] = jnp.broadcast_to(jnp.max(top, axis=1, keepdims=True), (ROWS, HEAD_DIM))
-
-    def weigh(y, blocks, scores, peaks):
-        peak = peaks[...]
-        size = blocks * PAIR
-        weights = [
-            jnp.exp2((scores[:, at : at + HEAD_DIM] - peak) * EXP2_SCALE).astype(jnp.bfloat16)
-            for at in range(0, size, HEAD_DIM)
-        ]
-        total = jnp.dot(
-            jnp.concatenate(weights, axis=1), values[:size, :], preferred_element_type=jnp.float32
-        )
-        mass = total[:, HEAD_DIM:]
-        out_ref[y, :ROWS, :] = (total[:, :HEAD_DIM] / mass).astype(jnp.bfloat16)
-        level = jnp.where(peak > 0.5 * NEG_FILL, peak * SCORE_SCALE + jnp.log(mass), NEG_FILL)
-        stat = jnp.zeros((STAT_ROWS, HEAD_DIM), jnp.float32)
-        row = iota((STAT_ROWS, HEAD_DIM), 0)
-        for k in range(ROWS // HEAD_DIM):
-            rest = row_of(level[k * HEAD_DIM : (k + 1) * HEAD_DIM])
-            for piece in range(3):
-                part = rest.astype(jnp.bfloat16).astype(jnp.float32)
-                stat = jnp.where(row == 3 * piece + k, part, stat)
-                rest = rest - part
-        out_ref[y, ROWS:, :] = stat.astype(jnp.bfloat16)
-
-    def all_groups(blocks, masked):
+        mass = total[HEAD_DIM : HEAD_DIM + 1]
+        outcome = (total[:HEAD_DIM] * (1.0 / mass)).astype(jnp.bfloat16)
+        rest = jnp.where(peak > 0.5 * NEG_FILL, peak * SCORE_SCALE + jnp.log(mass), NEG_FILL)
+        stat = jnp.zeros((STAT_ROWS, STEP), jnp.float32)
+        row = iota((STAT_ROWS, STEP), 0)
+        for piece in range(3):
+            part = rest.astype(jnp.bfloat16).astype(jnp.float32)
+            stat = jnp.where(row == piece, part, stat)
+            rest = rest - part
+        stat = stat.astype(jnp.bfloat16)
+        for half in range(STEP // HEAD_DIM):
+            tile = step * (STEP // HEAD_DIM) + half
+            y = tile // (ROWS // HEAD_DIM)
+            lanes = pl.ds(
+                pl.multiple_of(lax.rem(tile, ROWS // HEAD_DIM) * HEAD_DIM, HEAD_DIM), HEAD_DIM
+            )
+            columns = slice(half * HEAD_DIM, (half + 1) * HEAD_DIM)
+            out_ref[y, :HEAD_DIM, lanes] = outcome[:, columns]
+            out_ref[y, HEAD_DIM:, lanes] = stat[:, columns]
+
+    def all_steps(size, masked):
         even, odd = (scores_even, peaks_even), (scores_odd, peaks_odd)
-        score(0, blocks, masked, *even)
-
-        def step(pair, carry):
-            y = 2 * pair
-            score(y + 1, blocks, masked, *odd)
-            weigh(y, blocks, *even)
-            score(jnp.minimum(y + 2, Y - 1), blocks, masked, *even)
-            weigh(y + 1, blocks, *odd)
+        steps = Y * ROWS // STEP
+        score(0, size, masked, *even)
+        for part, (source, _) in enumerate(sources):
+            values[:HEAD_DIM, part * gathered : part * gathered + size] = source[:size, HEAD_DIM:].T
+        values[HEAD_DIM:, :] = jnp.ones((ONES, CORES * gathered), jnp.bfloat16)
+
+        def two(pair, carry):
+            step = 2 * pair
+            score(step + 1, size, masked, *odd)
+            weigh(step, size, *even)
+            score(step + 2, size, masked, *even)
+            weigh(step + 1, size, *odd)
             return carry
 
-        lax.fori_loop(0, Y // 2, step, 0)
+        lax.fori_loop(0, steps // 2 - 1, two, 0)
+        score(steps - 1, size, masked, *odd)
+        weigh(steps - 2, size, *even)
+        weigh(steps - 1, size, *odd)
 
     @pl.when(z_own == Z_HI - 1)
     def _():
-        all_groups(Z_HI, (Z_HI - 1,))
+        all_steps(gathered, gathered - GROUP_LEN)
 
     @pl.when(z_own != Z_HI - 1)
     def _():
-        all_groups(Z_HI - 1, tuple(range(Z_HI - 1)))
+        all_steps(SHORT, 0)
 
 
 def merge_kernel(count_ref, parts_ref, out_ref):
     live = iota((SLOTS, HEAD_DIM), 0) < count_ref[0]
-    eye = iota((HEAD_DIM, HEAD_DIM), 0) == iota((HEAD_DIM, HEAD_DIM), 1)
-    stats = [parts_ref[y, ROWS:, :].astype(jnp.float32) for y in range(Y)]
-    merged = []
+    levels = []
+    for y in range(Y):
+        stat = parts_ref[y, HEAD_DIM:, :].astype(jnp.float32)
+        levels.append(stat[0:1] + stat[1:2] + stat[2:3])
+    top = functools.reduce(jnp.maximum, levels)
+    shares = [jnp.exp(level - top) for level in levels]
+    scale = 1.0 / functools.reduce(jnp.add, shares)
     for k in range(ROWS // HEAD_DIM):
-        levels = [s[k : k + 1] + s[k + 3 : k + 4] + s[k + 6 : k + 7] for s in stats]
-        top = functools.reduce(jnp.maximum, levels)
-        shares = [jnp.exp(level - top) for level in levels]
-        whole = functools.reduce(jnp.add, shares)
+        lanes = slice(k * HEAD_DIM, (k + 1) * HEAD_DIM)
         total = jnp.zeros((HEAD_DIM, HEAD_DIM), jnp.float32)
         for y in range(Y):
-            share = jnp.broadcast_to(shares[y] / whole, (HEAD_DIM, HEAD_DIM))
-            share = jnp.sum(jnp.where(eye, share, 0.0), axis=1, keepdims=True)
-            part = parts_ref[y, k * HEAD_DIM : (k + 1) * HEAD_DIM, :].astype(jnp.float32)
-            total = total + share * part
-        merged.append(total)
-    merged = jnp.concatenate(merged, axis=0)
-    for h in range(HEADS_PER):
-        head = jnp.where(live, merged[h * SLOTS : (h + 1) * SLOTS], 0.0)
-        out_ref[:, h * HEAD_DIM : (h + 1) * HEAD_DIM] = head.astype(jnp.bfloat16)
+            part = parts_ref[y, :HEAD_DIM, lanes].astype(jnp.float32)
+            total = total + (shares[y] * scale)[:, lanes] * part
+        rows = total.T
+        for at in range(0, HEAD_DIM, 16):
+            head, slot = divmod(k * HEAD_DIM + at, SLOTS)
+            found = jnp.where(live[slot : slot + 16], rows[at : at + 16], 0.0)
+            out_ref[slot : slot + 16, head * HEAD_DIM : (head + 1) * HEAD_DIM] = found.astype(
+                jnp.bfloat16
+            )
 
 
 def kernel_params(mib):
@@ -295,7 +318,7 @@
             shape((1, SLOTS), f32),
         ),
         in_specs=[SMEM, SMEM, VMEM] + [HBM] * 6,
-        out_specs=[VMEM] * 5,
+        out_specs=[HBM] + [VMEM] * 4,
         scratch_shapes=[
             pltpu.VMEM((1, SLOTS), jnp.int32),
             pltpu.VMEM((SLOTS, HEADS_PER * HEAD_DIM), bf16),
@@ -303,7 +326,9 @@
             pltpu.VMEM((GROUP_LEN, HEAD_DIM), bf16),
             pltpu.VMEM((SLOTS, HEAD_DIM), bf16),
             pltpu.VMEM((SLOTS, HEAD_DIM), bf16),
+            pltpu.VMEM((ROWS, HEAD_DIM), bf16),
             pltpu.SemaphoreType.DMA((6,)),
+            pltpu.SemaphoreType.DMA((Y,)),
         ],
         name="prepare",
     )(
@@ -317,23 +342,24 @@
     core_kv = lax.all_gather(own_kv, "ctx", axis=0, axis_index_groups=KEY_GROUPS, tiled=True)
     other_kv = lax.ppermute(core_kv, "ctx", CORE_SWAP)
 
+    score_shape = pltpu.VMEM((CORES * Z_HI * GROUP_LEN, STEP), f32)
     partial = pl.pallas_call(
         attend_kernel,
-        out_shape=shape((Y, ROWS + STAT_ROWS, HEAD_DIM), bf16),
+        out_shape=shape((Y, HEAD_DIM + STAT_ROWS, ROWS), bf16),
         in_specs=[VMEM] * 4,
         out_specs=VMEM,
         scratch_shapes=[
-            pltpu.VMEM((Z_HI * PAIR, HEAD_DIM), bf16),
-            pltpu.VMEM((Z_HI * PAIR, 2 * HEAD_DIM), bf16),
-            pltpu.VMEM((ROWS, HEAD_DIM), f32),
-            pltpu.VMEM((ROWS, Z_HI * PAIR), f32),
-            pltpu.VMEM((ROWS, Z_HI * PAIR), f32),
-            pltpu.VMEM((ROWS, HEAD_DIM), f32),
-            pltpu.VMEM((ROWS, HEAD_DIM), f32),
+            pltpu.VMEM((HEAD_DIM + ONES, CORES * Z_HI * GROUP_LEN), bf16),
+            pltpu.VMEM((1, Y * ROWS), jnp.int32),
+            pltpu.VMEM((1, Y * ROWS), jnp.int32),
+            score_shape,
+            score_shape,
+            pltpu.VMEM((1, STEP), f32),
+            pltpu.VMEM((1, STEP), f32),
         ],
         compiler_params=kernel_params(28),
         name="attend",
-    )(recompute_index, all_queries, core_kv, other_kv)
+    )(recompute_index, all_queries.reshape(Y * ROWS, HEAD_DIM), core_kv, other_kv)
 
     parts = lax.all_to_all(
         partial, "ctx", 0, 0, axis_index_groups=QUERY_GROUPS, tiled=True

time: 83.7 us -> 83.2 us (level)
    pallas_call x1, Pallas kernels: 10.9 us -> 9.85 us  [shards(): pl.pallas_call(attend_kernel, out_shape=shape((Y, HEAD_DIM + STAT_ROWS, R...]
where the time goes in v3:
time: 83.2 us; the launch traced here: 82.9 us
  blocking collectives  37.3 us (45%)
  starting transfers between devices  19.1 us (23%)
  Pallas kernels  14.2 us (17%)
  waiting for transfers between devices  9.22 us (11%)
  between operations  1.32 us (2%)
  other arithmetic  1.15 us (1%)
    all_gather x1, blocking collectives, shards(): lax.all_gather(own_kv, 'ctx', axis=0, axis_index_groups=KEY_GROUPS, tiled...  21.4 us
    all_gather x1, blocking collectives, shards(): squares = lax.all_gather(squares, 'head', axis=0, tiled=True)  15.9 us
    pallas_call x1, Pallas kernels, shards(): pl.pallas_call(attend_kernel, out_shape=shape((Y, HEAD_DIM + STAT_ROWS, R...  9.85 us
    all_to_all x1, starting transfers between devices, shards(): lax.all_to_all(copies, 'ctx', 0, 0, axis_index_groups=QUERY_GROUPS, tiled...  7.78 us
    all_to_all x1, waiting for transfers between devices, shards(): lax.all_to_all(partial, 'ctx', 0, 0, axis_index_groups=QUERY_GROUPS, tile...  7.52 us
    all_to_all x1, starting transfers between devices, shards(): lax.all_to_all(partial, 'ctx', 0, 0, axis_index_groups=QUERY_GROUPS, tile...  7.26 us
    ppermute x1, starting transfers between devices, shards(): other_kv = lax.ppermute(core_kv, 'ctx', CORE_SWAP)  4.03 us
    pallas_call x1, Pallas kernels, shards(): pl.pallas_call(prepare_kernel, out_shape=(shape((Y, ROWS, HEAD_DIM), bf16...  3.41 us
  transfers between devices with their start and end apart: 3, of which 2 were waited for; matrix products, arithmetic and copies ran while one was open for 1% of the time, Pallas kernels for 0%

profile of v3, /device:TPU:1, one launch (start us, length us, event | category | flops | bytes accessed | tf_op | source)
XLA Modules:
  0.0 82.9 jit_solution(16335627339205158722)
XLA Ops:
  1.3 0.6 maximum_bitcast_fusion.freq_ref
  1.9 3.4 %prepare.1 = (bf16[8,384,128]{2,1,0:T(8,128)(2,1)}, bf16[320,256]{1,0:T(8,128)(2,1)}, bf16[320,128]{1,0:T(8,128)(2,1)}, bf16[320,128]{1,0:T(8,128)(2,1)}, f32[1,48]{1,0:T(1,128)}) custom-call(s32[64]{0:T(128)} %offsets.1, s32[1]{0:T(128)} %copy.12.count_ref, f32[1,128]{1,0:T(1,128)} %maximum_bitcast_fusion.freq_ref, s32[1,48]{1,0:T(1,128)} %index_ref.1, ...), custom_call_target="tpu_custom_call" | custom-call | tf_op jit(solution)/shard_map/prepare/pallas_call | solution.py:311
  5.3 0.0 copy-start.1
  5.3 7.8 %all-to-all-start = ((bf16[8,384,128]{2,1,0:T(8,128)(2,1)}), bf16[8,384,128]{2,1,0:T(8,128)(2,1)S(1)}, u32[]{:S(2)}, u32[]{:S(2)}) async-start(bf16[8,384,128]{2,1,0:T(8,128)(2,1)} %get-tuple-element.9), calls=%async_computation | async-start | bytes 1572864 | tf_op jit(solution)/shard_map/all_to_all | solution.py:339
  13.1 0.0 copy-done.1
  13.1 21.4 %all_gather.6.own_ref = bf16[1280,256]{1,0:T(8,128)(2,1)S(1)} all-gather(bf16[320,256]{1,0:T(8,128)(2,1)S(1)} %copy-done.1), channel_id=1, replica_groups={{0,128,256,384},{8,136,264,392},{16,144,272,400},{24,152,280,408},{32,1..., dimensions={0}, use_global_device_ids=true | all-gather | bytes 819200 | tf_op jit(solution)/shard_map/all_gather | solution.py:342
  34.5 0.0 copy-start
  34.5 4.0 %collective-permute-start = (bf16[1280,256]{1,0:T(8,128)(2,1)S(1)}, bf16[1280,256]{1,0:T(8,128)(2,1)S(1)}, u32[]{:S(2)}, u32[]{:S(2)}) collective-permute-start(bf16[1280,256]{1,0:T(8,128)(2,1)S(1)} %all_gather.6.own_ref), channel_id=1, source_target_pairs={{0,8},{8,0},{16,24},{24,16},{32,40},{40,32},{48,56},{56,48},{64,72... | collective-permute-start | bytes 1966088 | tf_op jit(solution)/shard_map/ppermute | solution.py:343
  38.5 1.7 %collective-permute-done.other_ref = bf16[1280,256]{1,0:T(8,128)(2,1)S(1)} collective-permute-done((bf16[1280,256]{1,0:T(8,128)(2,1)S(1)}, bf16[1280,256]{1,0:T(8,128)(2,1)S(1)}, u32[]{:S(2)}, u32[]{:S(2)}) %collective-permute-start) | collective-permute-done | bytes 655392 | tf_op jit(solution)/shard_map/ppermute | solution.py:343
  40.2 0.0 all-to-all-done
  40.2 0.0 copy-done
  40.2 9.9 %attend.1 = bf16[8,136,384]{2,1,0:T(8,128)(2,1)} custom-call(s32[1,48]{1,0:T(1,128)S(1)} %copy-done, bf16[3072,128]{1,0:T(8,128)(2,1)S(1)} %bitcast.8, bf16[1280,256]{1,0:T(8,128)(2,1)S(1)} %all_gather.6.own_ref, bf16[1280,256]{1,0:T(8,128)(2,1)S(1)} %collective-permute-done.other_ref), custom_call_target="tpu_custom_call" | custom-call | tf_op jit(solution)/shard_map/attend/pallas_call | solution.py:346
  50.1 7.3 %all-to-all-start.1 = ((bf16[8,136,384]{2,1,0:T(8,128)(2,1)}), bf16[8,136,384]{2,1,0:T(8,128)(2,1)S(1)}, u32[]{:S(2)}, u32[]{:S(2)}) async-start(bf16[8,136,384]{2,1,0:T(8,128)(2,1)} %attend.1), calls=%async_computation.1 | async-start | bytes 1671168 | tf_op jit(solution)/shard_map/all_to_all | solution.py:364
  57.3 0.0 copy-start.2
  57.3 0.7 copy-done.2
  58.0 15.9 %all-gather = f32[8,1,48]{2,1,0:T(1,128)S(1)} all-gather(f32[1,1,48]{2,1,0:T(1,128)S(1)} %bitcast.9), channel_id=1, replica_groups=mesh['ctx'=64,'head'=8] {'head'}, dimensions={0}, use_global_device_ids=true | all-gather | bytes 1728 | tf_op jit(solution)/shard_map/all_gather | solution.py:367
  73.9 0.5 compare_select_fusion
  74.4 7.5 %all-to-all-done.1.parts_ref = bf16[8,136,384]{2,1,0:T(8,128)(2,1)S(1)} async-done(((bf16[8,136,384]{2,1,0:T(8,128)(2,1)}), bf16[8,136,384]{2,1,0:T(8,128)(2,1)S(1)}, u32[]{:S(2)}, u32[]{:S(2)}) %all-to-all-start.1) | async-done | bytes 835616 | tf_op jit(solution)/shard_map/all_to_all | solution.py:364
  81.9 0.9 %merge.1 = bf16[48,1024]{1,0:T(8,128)(2,1)} custom-call(s32[1]{0:T(128)} %copy.12.count_ref, bf16[8,136,384]{2,1,0:T(8,128)(2,1)S(1)} %all-to-all-done.1.parts_ref), custom_call_target="tpu_custom_call" | custom-call | tf_op jit(solution)/shard_map/merge/pallas_call | solution.py:372
  (2 shorter events, 0.0 us)
Async XLA Ops:
  5.3 7.8 %copy-start.1 = (bf16[320,256]{1,0:T(8,128)(2,1)S(1)}, bf16[320,256]{1,0:T(8,128)(2,1)}, u32[]{:S(2)}) copy-start(bf16[320,256]{1,0:T(8,128)(2,1)} %get-tuple-element.10) | copy-start | bytes 491524
  5.3 34.9 %all-to-all-start = ((bf16[8,384,128]{2,1,0:T(8,128)(2,1)}), bf16[8,384,128]{2,1,0:T(8,128)(2,1)S(1)}, u32[]{:S(2)}, u32[]{:S(2)}) async-start(bf16[8,384,128]{2,1,0:T(8,128)(2,1)} %get-tuple-element.9), calls=%async_computation | async-start | bytes 1572864 | tf_op jit(solution)/shard_map/all_to_all | solution.py:339
  34.5 5.7 %copy-start = (s32[1,48]{1,0:T(1,128)S(1)}, s32[1,48]{1,0:T(1,128)}, u32[]{:S(2)}) copy-start(s32[1,48]{1,0:T(1,128)} %index_ref.1) | copy-start | bytes 580
  34.5 5.7 %collective-permute-start = (bf16[1280,256]{1,0:T(8,128)(2,1)S(1)}, bf16[1280,256]{1,0:T(8,128)(2,1)S(1)}, u32[]{:S(2)}, u32[]{:S(2)}) collective-permute-start(bf16[1280,256]{1,0:T(8,128)(2,1)S(1)} %all_gather.6.own_ref), channel_id=1, source_target_pairs={{0,8},{8,0},{16,24},{24,16},{32,40},{40,32},{48,56},{56,48},{64,72... | collective-permute-start | bytes 1966088 | tf_op jit(solution)/shard_map/ppermute | solution.py:343
  50.1 31.9 %all-to-all-start.1 = ((bf16[8,136,384]{2,1,0:T(8,128)(2,1)}), bf16[8,136,384]{2,1,0:T(8,128)(2,1)S(1)}, u32[]{:S(2)}, u32[]{:S(2)}) async-start(bf16[8,136,384]{2,1,0:T(8,128)(2,1)} %attend.1), calls=%async_computation.1 | async-start | bytes 1671168 | tf_op jit(solution)/shard_map/all_to_all | solution.py:364
  57.3 0.7 copy-start.2

commit v4 on v3

--- a/solution.py
+++ b/solution.py
@@ -36,7 +36,10 @@
     return (z_hi * Y + y) * CORES + core
 
 
-QUERY_GROUPS = [[ctx_index(z, y, c) for y in range(Y)] for z in range(Z_HI) for c in range(CORES)]
+QUERY_ORDERS = [list(range(Y)), list(range(Y - 1, -1, -1))]
+QUERY_GROUPS = [
+    [ctx_index(z, y, c) for y in QUERY_ORDERS[c]] for z in range(Z_HI) for c in range(CORES)
+]
 KEY_GROUPS = [[ctx_index(z, y, c) for z in range(Z_HI)] for y in range(Y) for c in range(CORES)]
 CORE_SWAP = [(i, i ^ 1) for i in range(Z_HI * Y * CORES)]
 
@@ -74,7 +77,7 @@
 def prepare_kernel(
     offsets, count_ref, freq_ref, index_hbm, q_hbm, ck_hbm, cv_hbm, fk_hbm, fv_hbm,
     q_out, kv_out, jk_out, jv_out, drift_out,
-    index_ref, q_ref, ck_ref, cv_ref, fk_ref, fv_ref, turned_q, arrived, left,
+    index_ref, q_ref, ck_ref, cv_ref, fk_ref, fv_ref, arrived,
 ):
     copies = [
         pltpu.make_async_copy(source, target, arrived.at[i])
@@ -106,10 +109,8 @@
     copies[1].wait()
     for h in range(HEADS_PER):
         head = turn(q_ref[:, h * HEAD_DIM : (h + 1) * HEAD_DIM], slot_cos, slot_sin)
-        turned_q[h * SLOTS : (h + 1) * SLOTS, :] = head
-    sends = [pltpu.make_async_copy(turned_q, q_out.at[y], left.at[y]) for y in range(Y)]
-    for send in sends:
-        send.start()
+        for y in range(Y):
+            q_out[y, h * SLOTS : (h + 1) * SLOTS, :] = head
 
     for copy in copies[2:]:
         copy.wait()
@@ -150,8 +151,6 @@
     squares = jnp.sum(key_gap * key_gap + value_gap * value_gap, axis=1, keepdims=True)
     drift_row = row_of(jnp.broadcast_to(squares, (SLOTS, SLOTS)))
     drift_out[...] = drift_row
-    for send in sends:
-        send.wait()
 
 
 def attend_kernel(
@@ -172,8 +171,9 @@
     )
     before = z_own * GROUP_LEN - 1
     full = before + GROUP_LEN
-    for y in range(Y):
-        lanes = slice(y * ROWS, (y + 1) * ROWS)
+    for place in range(Y):
+        y = jnp.where(core == 1, QUERY_ORDERS[1][place], QUERY_ORDERS[0][place])
+        lanes = slice(place * ROWS, (place + 1) * ROWS)
         beside = jnp.where(y_own < y, full, before)
         own_limit[:, lanes] = jnp.where(
             y == y_own, own_index.astype(jnp.int32) + (before + 1), beside
@@ -228,13 +228,13 @@
         stat = stat.astype(jnp.bfloat16)
         for half in range(STEP // HEAD_DIM):
             tile = step * (STEP // HEAD_DIM) + half
-            y = tile // (ROWS // HEAD_DIM)
+            place = tile // (ROWS // HEAD_DIM)
             lanes = pl.ds(
                 pl.multiple_of(lax.rem(tile, ROWS // HEAD_DIM) * HEAD_DIM, HEAD_DIM), HEAD_DIM
             )
             columns = slice(half * HEAD_DIM, (half + 1) * HEAD_DIM)
-            out_ref[y, :HEAD_DIM, lanes] = outcome[:, columns]
-            out_ref[y, HEAD_DIM:, lanes] = stat[:, columns]
+            out_ref[place, :HEAD_DIM, lanes] = outcome[:, columns]
+            out_ref[place, HEAD_DIM:, lanes] = stat[:, columns]
 
     def all_steps(size, masked):
         even, odd = (scores_even, peaks_even), (scores_odd, peaks_odd)
@@ -318,7 +318,7 @@
             shape((1, SLOTS), f32),
         ),
         in_specs=[SMEM, SMEM, VMEM] + [HBM] * 6,
-        out_specs=[HBM] + [VMEM] * 4,
+        out_specs=[VMEM] * 5,
         scratch_shapes=[
             pltpu.VMEM((1, SLOTS), jnp.int32),
             pltpu.VMEM((SLOTS, HEADS_PER * HEAD_DIM), bf16),
@@ -326,9 +326,7 @@
             pltpu.VMEM((GROUP_LEN, HEAD_DIM), bf16),
             pltpu.VMEM((SLOTS, HEAD_DIM), bf16),
             pltpu.VMEM((SLOTS, HEAD_DIM), bf16),
-            pltpu.VMEM((ROWS, HEAD_DIM), bf16),
             pltpu.SemaphoreType.DMA((6,)),
-            pltpu.SemaphoreType.DMA((Y,)),
         ],
         name="prepare",
     )(

time: 83.2 us -> 78.9 us (0.948)
  the two profiles are of different devices: /device:TPU:1 before, /device:TPU:78 now
where the time goes in v4:
time: 78.9 us; the launch traced here: 78.5 us
  blocking collectives  36.8 us (47%)
  starting transfers between devices  18.1 us (23%)
  Pallas kernels  13.6 us (17%)
  waiting for transfers between devices  6.93 us (9%)
  between operations  1.32 us (2%)
  other arithmetic  1.15 us (1%)
    all_gather x1, blocking collectives, shards(): lax.all_gather(own_kv, 'ctx', axis=0, axis_index_groups=KEY_GROUPS, tiled...  22 us
    all_gather x1, blocking collectives, shards(): squares = lax.all_gather(squares, 'head', axis=0, tiled=True)  14.8 us
    pallas_call x1, Pallas kernels, shards(): pl.pallas_call(attend_kernel, out_shape=shape((Y, HEAD_DIM + STAT_ROWS, R...  9.85 us
    all_to_all x1, starting transfers between devices, shards(): lax.all_to_all(partial, 'ctx', 0, 0, axis_index_groups=QUERY_GROUPS, tile...  8.34 us
    all_to_all x1, starting transfers between devices, shards(): lax.all_to_all(copies, 'ctx', 0, 0, axis_index_groups=QUERY_GROUPS, tiled...  7.69 us
    all_to_all x1, waiting for transfers between devices, shards(): lax.all_to_all(partial, 'ctx', 0, 0, axis_index_groups=QUERY_GROUPS, tile...  4.86 us
    pallas_call x1, Pallas kernels, shards(): pl.pallas_call(prepare_kernel, out_shape=(shape((Y, ROWS, HEAD_DIM), bf16...  2.84 us
    ppermute x1, waiting for transfers between devices, shards(): other_kv = lax.ppermute(core_kv, 'ctx', CORE_SWAP)  2.06 us
  transfers between devices with their start and end apart: 3, of which 2 were waited for; matrix products, arithmetic and copies ran while one was open for 1% of the time, Pallas kernels for 0%

profile of v4, /device:TPU:78, one launch (start us, length us, event | category | flops | bytes accessed | tf_op | source)
XLA Modules:
  0.0 78.5 jit_solution(10426650662302680573)
XLA Ops:
  1.3 0.6 maximum_bitcast_fusion.freq_ref
  1.9 2.8 %prepare.1 = (bf16[8,384,128]{2,1,0:T(8,128)(2,1)}, bf16[320,256]{1,0:T(8,128)(2,1)}, bf16[320,128]{1,0:T(8,128)(2,1)}, bf16[320,128]{1,0:T(8,128)(2,1)}, f32[1,48]{1,0:T(1,128)}) custom-call(s32[64]{0:T(128)} %offsets.1, s32[1]{0:T(128)} %copy.12.count_ref, f32[1,128]{1,0:T(1,128)} %maximum_bitcast_fusion.freq_ref, s32[1,48]{1,0:T(1,128)} %index_ref.1, ...), custom_call_target="tpu_custom_call" | custom-call | tf_op jit(solution)/shard_map/prepare/pallas_call | solution.py:311
  4.7 0.0 copy-start.1
  4.8 7.7 %all-to-all-start = ((bf16[8,384,128]{2,1,0:T(8,128)(2,1)}), bf16[8,384,128]{2,1,0:T(8,128)(2,1)S(1)}, u32[]{:S(2)}, u32[]{:S(2)}) async-start(bf16[8,384,128]{2,1,0:T(8,128)(2,1)} %get-tuple-element.9), calls=%async_computation | async-start | bytes 1572864 | tf_op jit(solution)/shard_map/all_to_all | solution.py:337
  12.4 0.0 copy-done.1
  12.4 22.0 %all_gather.6.own_ref = bf16[1280,256]{1,0:T(8,128)(2,1)S(1)} all-gather(bf16[320,256]{1,0:T(8,128)(2,1)S(1)} %copy-done.1), channel_id=1, replica_groups={{0,128,256,384},{8,136,264,392},{16,144,272,400},{24,152,280,408},{32,1..., dimensions={0}, use_global_device_ids=true | all-gather | bytes 819200 | tf_op jit(solution)/shard_map/all_gather | solution.py:340
  34.4 0.0 copy-start
  34.4 2.0 %collective-permute-start = (bf16[1280,256]{1,0:T(8,128)(2,1)S(1)}, bf16[1280,256]{1,0:T(8,128)(2,1)S(1)}, u32[]{:S(2)}, u32[]{:S(2)}) collective-permute-start(bf16[1280,256]{1,0:T(8,128)(2,1)S(1)} %all_gather.6.own_ref), channel_id=1, source_target_pairs={{0,8},{8,0},{16,24},{24,16},{32,40},{40,32},{48,56},{56,48},{64,72... | collective-permute-start | bytes 1966088 | tf_op jit(solution)/shard_map/ppermute | solution.py:341
  36.5 2.1 %collective-permute-done.other_ref = bf16[1280,256]{1,0:T(8,128)(2,1)S(1)} collective-permute-done((bf16[1280,256]{1,0:T(8,128)(2,1)S(1)}, bf16[1280,256]{1,0:T(8,128)(2,1)S(1)}, u32[]{:S(2)}, u32[]{:S(2)}) %collective-permute-start) | collective-permute-done | bytes 655392 | tf_op jit(solution)/shard_map/ppermute | solution.py:341
  38.5 0.0 all-to-all-done
  38.5 0.0 copy-done
  38.5 9.9 %attend.1 = bf16[8,136,384]{2,1,0:T(8,128)(2,1)} custom-call(s32[1,48]{1,0:T(1,128)S(1)} %copy-done, bf16[3072,128]{1,0:T(8,128)(2,1)S(1)} %bitcast.8, bf16[1280,256]{1,0:T(8,128)(2,1)S(1)} %all_gather.6.own_ref, bf16[1280,256]{1,0:T(8,128)(2,1)S(1)} %collective-permute-done.other_ref), custom_call_target="tpu_custom_call" | custom-call | tf_op jit(solution)/shard_map/attend/pallas_call | solution.py:344
  48.4 8.3 %all-to-all-start.1 = ((bf16[8,136,384]{2,1,0:T(8,128)(2,1)}), bf16[8,136,384]{2,1,0:T(8,128)(2,1)S(1)}, u32[]{:S(2)}, u32[]{:S(2)}) async-start(bf16[8,136,384]{2,1,0:T(8,128)(2,1)} %attend.1), calls=%async_computation.1 | async-start | bytes 1671168 | tf_op jit(solution)/shard_map/all_to_all | solution.py:362
  56.7 0.0 copy-start.2
  56.7 0.7 copy-done.2
  57.4 14.8 %all-gather = f32[8,1,48]{2,1,0:T(1,128)S(1)} all-gather(f32[1,1,48]{2,1,0:T(1,128)S(1)} %bitcast.9), channel_id=1, replica_groups=mesh['ctx'=64,'head'=8] {'head'}, dimensions={0}, use_global_device_ids=true | all-gather | bytes 1728 | tf_op jit(solution)/shard_map/all_gather | solution.py:365
  72.2 0.5 compare_select_fusion
  72.7 4.9 %all-to-all-done.1.parts_ref = bf16[8,136,384]{2,1,0:T(8,128)(2,1)S(1)} async-done(((bf16[8,136,384]{2,1,0:T(8,128)(2,1)}), bf16[8,136,384]{2,1,0:T(8,128)(2,1)S(1)}, u32[]{:S(2)}, u32[]{:S(2)}) %all-to-all-start.1) | async-done | bytes 835616 | tf_op jit(solution)/shard_map/all_to_all | solution.py:362
  77.6 0.9 %merge.1 = bf16[48,1024]{1,0:T(8,128)(2,1)} custom-call(s32[1]{0:T(128)} %copy.12.count_ref, bf16[8,136,384]{2,1,0:T(8,128)(2,1)S(1)} %all-to-all-done.1.parts_ref), custom_call_target="tpu_custom_call" | custom-call | tf_op jit(solution)/shard_map/merge/pallas_call | solution.py:370
  (2 shorter events, 0.0 us)
Async XLA Ops:
  4.7 7.7 %copy-start.1 = (bf16[320,256]{1,0:T(8,128)(2,1)S(1)}, bf16[320,256]{1,0:T(8,128)(2,1)}, u32[]{:S(2)}) copy-start(bf16[320,256]{1,0:T(8,128)(2,1)} %get-tuple-element.10) | copy-start | bytes 491524
  4.8 33.8 %all-to-all-start = ((bf16[8,384,128]{2,1,0:T(8,128)(2,1)}), bf16[8,384,128]{2,1,0:T(8,128)(2,1)S(1)}, u32[]{:S(2)}, u32[]{:S(2)}) async-start(bf16[8,384,128]{2,1,0:T(8,128)(2,1)} %get-tuple-element.9), calls=%async_computation | async-start | bytes 1572864 | tf_op jit(solution)/shard_map/all_to_all | solution.py:337
  34.4 4.1 %copy-start = (s32[1,48]{1,0:T(1,128)S(1)}, s32[1,48]{1,0:T(1,128)}, u32[]{:S(2)}) copy-start(s32[1,48]{1,0:T(1,128)} %index_ref.1) | copy-start | bytes 580
  34.4 4.1 %collective-permute-start = (bf16[1280,256]{1,0:T(8,128)(2,1)S(1)}, bf16[1280,256]{1,0:T(8,128)(2,1)S(1)}, u32[]{:S(2)}, u32[]{:S(2)}) collective-permute-start(bf16[1280,256]{1,0:T(8,128)(2,1)S(1)} %all_gather.6.own_ref), channel_id=1, source_target_pairs={{0,8},{8,0},{16,24},{24,16},{32,40},{40,32},{48,56},{56,48},{64,72... | collective-permute-start | bytes 1966088 | tf_op jit(solution)/shard_map/ppermute | solution.py:341
  48.4 29.2 %all-to-all-start.1 = ((bf16[8,136,384]{2,1,0:T(8,128)(2,1)}), bf16[8,136,384]{2,1,0:T(8,128)(2,1)S(1)}, u32[]{:S(2)}, u32[]{:S(2)}) async-start(bf16[8,136,384]{2,1,0:T(8,128)(2,1)} %attend.1), calls=%async_computation.1 | async-start | bytes 1671168 | tf_op jit(solution)/shard_map/all_to_all | solution.py:362
  56.7 0.7 copy-start.2

commit v5 on v4

--- a/solution.py
+++ b/solution.py
@@ -3,6 +3,7 @@
 
 import jax
 import jax.numpy as jnp
+import numpy as np
 from jax import lax
 from jax.experimental import pallas as pl
 from jax.experimental.pallas import tpu as pltpu
@@ -45,17 +46,12 @@
 
 
 def inverse_freq():
-    half_dim = HEAD_DIM // 2
-    exponent = jnp.arange(half_dim, dtype=jnp.float32) * 2.0 / HEAD_DIM
-    base_freq = 1.0 / 500000.0**exponent
-    wavelength = 2.0 * jnp.pi / base_freq
+    base = 1.0 / 500000.0 ** (np.arange(HEAD_DIM // 2) * 2.0 / HEAD_DIM)
+    wavelength = 2.0 * np.pi / base
     smooth = (8192.0 / wavelength - 1.0) / 3.0
-    blended_freq = (1.0 - smooth) * base_freq / 8.0 + smooth * base_freq
-    return jnp.where(
-        wavelength < 2048.0,
-        base_freq,
-        jnp.where(wavelength > 8192.0, base_freq / 8.0, blended_freq),
-    )
+    blended = (1.0 - smooth) * base / 8.0 + smooth * base
+    freq = np.where(wavelength < 2048.0, base, np.where(wavelength > 8192.0, base / 8.0, blended))
+    return [float(value) for value in freq.astype(np.float32)]
 
 
 def iota(shape, dim):
@@ -75,9 +71,9 @@
 
 
 def prepare_kernel(
-    offsets, count_ref, freq_ref, index_hbm, q_hbm, ck_hbm, cv_hbm, fk_hbm, fv_hbm,
+    offsets, count_ref, index_hbm, q_hbm, ck_hbm, cv_hbm, fk_hbm, fv_hbm,
     q_out, kv_out, jk_out, jv_out, drift_out,
-    index_ref, q_ref, ck_ref, cv_ref, fk_ref, fv_ref, arrived,
+    index_ref, q_ref, ck_ref, cv_ref, fk_ref, fv_ref, copies_ref, kv_ref, drift_ref, arrived, left,
 ):
     copies = [
         pltpu.make_async_copy(source, target, arrived.at[i])
@@ -88,13 +84,26 @@
     ]
     for copy in copies:
         copy.start()
-    copies[0].wait()
+    sends = [
+        pltpu.make_async_copy(source, target, left.at[i])
+        for i, (source, target) in enumerate((
+            (copies_ref, q_out),
+            (kv_ref, kv_out),
+            (kv_ref.at[:, :HEAD_DIM], jk_out),
+            (kv_ref.at[:, HEAD_DIM:], jv_out),
+            (drift_ref, drift_out),
+        ))
+    ]
+    half = HEAD_DIM // 2
+    lane = lax.rem(iota((1, HEAD_DIM), 1), half)
+    freq = jnp.zeros((1, HEAD_DIM), jnp.float32)
+    for i, value in enumerate(inverse_freq()):
+        freq = jnp.where(lane == i, value, freq)
     own_start = offsets[lax.axis_index("ctx")]
     count = count_ref[0]
-    half = HEAD_DIM // 2
+    copies[0].wait()
     index_row = index_ref[...]
     index_col = column_of(index_row.astype(jnp.float32))
-    freq = freq_ref[...]
     start_row = jnp.full((1, HEAD_DIM), own_start, jnp.int32).astype(jnp.float32)
     slot_angle = (index_col + start_row[:, :1]) * freq
     group_angle = start_row * freq
@@ -110,7 +119,8 @@
     for h in range(HEADS_PER):
         head = turn(q_ref[:, h * HEAD_DIM : (h + 1) * HEAD_DIM], slot_cos, slot_sin)
         for y in range(Y):
-            q_out[y, h * SLOTS : (h + 1) * SLOTS, :] = head
+            copies_ref[y, h * SLOTS : (h + 1) * SLOTS, :] = head
+    sends[0].start()
 
     for copy in copies[2:]:
         copy.wait()
@@ -134,10 +144,10 @@
         jnp.dot(picker, fresh_values, preferred_element_type=jnp.float32),
         cached_values.astype(jnp.float32),
     ).astype(jnp.bfloat16)
-    jk_out[...] = joined_keys
-    jv_out[...] = joined_values
-    kv_out[:, :HEAD_DIM] = joined_keys
-    kv_out[:, HEAD_DIM:] = joined_values
+    kv_ref[:, :HEAD_DIM] = joined_keys
+    kv_ref[:, HEAD_DIM:] = joined_values
+    for send in sends[1:4]:
+        send.start()
 
     reader = jnp.where(
         iota((SLOTS, GROUP_LEN), 1).astype(jnp.float32) == index_col, 1.0, 0.0
@@ -150,12 +160,15 @@
     )
     squares = jnp.sum(key_gap * key_gap + value_gap * value_gap, axis=1, keepdims=True)
     drift_row = row_of(jnp.broadcast_to(squares, (SLOTS, SLOTS)))
-    drift_out[...] = drift_row
+    drift_ref[...] = drift_row
+    sends[4].start()
+    for send in sends:
+        send.wait()
 
 
 def attend_kernel(
-    index_ref, q_ref, own_ref, other_ref, out_ref, values, own_limit, other_limit,
-    scores_even, scores_odd, peaks_even, peaks_odd,
+    index_ref, q_ref, own_ref, other_ref, out_hbm, values, own_limit, other_limit,
+    scores_even, scores_odd, peaks_even, peaks_odd, out_ref, left,
 ):
     me = lax.axis_index("ctx")
     core = lax.rem(me, CORES)
@@ -253,9 +266,16 @@
             return carry
 
         lax.fori_loop(0, steps // 2 - 1, two, 0)
+        done = (steps - 2) * STEP // ROWS
+        first = pltpu.make_async_copy(out_ref.at[:done], out_hbm.at[:done], left.at[0])
+        first.start()
         score(steps - 1, size, masked, *odd)
         weigh(steps - 2, size, *even)
         weigh(steps - 1, size, *odd)
+        last = pltpu.make_async_copy(out_ref.at[done:], out_hbm.at[done:], left.at[1])
+        last.start()
+        first.wait()
+        last.wait()
 
     @pl.when(z_own == Z_HI - 1)
     def _():
@@ -306,8 +326,6 @@
 ):
     bf16, f32 = jnp.bfloat16, jnp.float32
     shape = jax.ShapeDtypeStruct
-    freq = inverse_freq()
-    freq = jnp.concatenate([freq, freq])[None, :]
     copies, own_kv, joined_keys, joined_values, squares = pl.pallas_call(
         prepare_kernel,
         out_shape=(
@@ -317,8 +335,8 @@
             shape((GROUP_LEN, HEAD_DIM), bf16),
             shape((1, SLOTS), f32),
         ),
-        in_specs=[SMEM, SMEM, VMEM] + [HBM] * 6,
-        out_specs=[VMEM] * 5,
+        in_specs=[SMEM, SMEM] + [HBM] * 6,
+        out_specs=[HBM] * 5,
         scratch_shapes=[
             pltpu.VMEM((1, SLOTS), jnp.int32),
             pltpu.VMEM((SLOTS, HEADS_PER * HEAD_DIM), bf16),
@@ -326,11 +344,15 @@
             pltpu.VMEM((GROUP_LEN, HEAD_DIM), bf16),
             pltpu.VMEM((SLOTS, HEAD_DIM), bf16),
             pltpu.VMEM((SLOTS, HEAD_DIM), bf16),
+            pltpu.VMEM((Y, ROWS, HEAD_DIM), bf16),
+            pltpu.VMEM((GROUP_LEN, 2 * HEAD_DIM), bf16),
+            pltpu.VMEM((1, SLOTS), f32),
             pltpu.SemaphoreType.DMA((6,)),
+            pltpu.SemaphoreType.DMA((5,)),
         ],
         name="prepare",
     )(
-        group_offsets, recompute_count, freq, recompute_index,
+        group_offsets, recompute_count, recompute_index,
         queries, cached_keys, cached_values, fresh_keys, fresh_values,
     )
 
@@ -345,7 +367,7 @@
         attend_kernel,
         out_shape=shape((Y, HEAD_DIM + STAT_ROWS, ROWS), bf16),
         in_specs=[VMEM] * 4,
-        out_specs=VMEM,
+        out_specs=HBM,
         scratch_shapes=[
             pltpu.VMEM((HEAD_DIM + ONES, CORES * Z_HI * GROUP_LEN), bf16),
             pltpu.VMEM((1, Y * ROWS), jnp.int32),
@@ -354,6 +376,8 @@
             score_shape,
             pltpu.VMEM((1, STEP), f32),
             pltpu.VMEM((1, STEP), f32),
+            pltpu.VMEM((Y, HEAD_DIM + STAT_ROWS, ROWS), bf16),
+            pltpu.SemaphoreType.DMA((2,)),
         ],
         compiler_params=kernel_params(28),
         name="attend",

time: 78.9 us -> 78.1 us (0.990)
  the two profiles are of different devices: /device:TPU:78 before, /device:TPU:76 now
where the time goes in v5:
time: 78.1 us; the launch traced here: 77.8 us
  blocking collectives  36.1 us (46%)
  starting transfers between devices  18.1 us (23%)
  Pallas kernels  13.4 us (17%)
  waiting for transfers between devices  7.61 us (10%)
  between operations  1.32 us (2%)
    all_gather x1, blocking collectives, shards(): lax.all_gather(own_kv, 'ctx', axis=0, axis_index_groups=KEY_GROUPS, tiled...  22 us
    all_gather x1, blocking collectives, shards(): squares = lax.all_gather(squares, 'head', axis=0, tiled=True)  14.2 us
    pallas_call x1, Pallas kernels, shards(): pl.pallas_call(attend_kernel, out_shape=shape((Y, HEAD_DIM + STAT_ROWS, R...  9.66 us
    all_to_all x1, starting transfers between devices, shards(): lax.all_to_all(partial, 'ctx', 0, 0, axis_index_groups=QUERY_GROUPS, tile...  8.34 us
    all_to_all x1, starting transfers between devices, shards(): lax.all_to_all(copies, 'ctx', 0, 0, axis_index_groups=QUERY_GROUPS, tiled...  7.69 us
    all_to_all x1, waiting for transfers between devices, shards(): lax.all_to_all(partial, 'ctx', 0, 0, axis_index_groups=QUERY_GROUPS, tile...  5.54 us
    pallas_call x1, Pallas kernels, shards(): pl.pallas_call(prepare_kernel, out_shape=(shape((Y, ROWS, HEAD_DIM), bf16...  2.88 us
    ppermute x1, waiting for transfers between devices, shards(): other_kv = lax.ppermute(core_kv, 'ctx', CORE_SWAP)  2.06 us
  transfers between devices with their start and end apart: 3, of which 2 were waited for; matrix products, arithmetic and copies ran while one was open for 1% of the time, Pallas kernels for 0%

profile of v5, /device:TPU:76, one launch (start us, length us, event | category | flops | bytes accessed | tf_op | source)
XLA Modules:
  0.0 77.8 jit_solution(8718810719052362914)
XLA Ops:
  1.3 2.9 %prepare.1 = (bf16[8,384,128]{2,1,0:T(8,128)(2,1)}, bf16[320,256]{1,0:T(8,128)(2,1)}, bf16[320,128]{1,0:T(8,128)(2,1)}, bf16[320,128]{1,0:T(8,128)(2,1)}, f32[1,48]{1,0:T(1,128)}) custom-call(s32[64]{0:T(128)} %offsets.1, s32[1]{0:T(128)} %copy.12.count_ref, s32[1,48]{1,0:T(1,128)} %index_ref.1, bf16[48,1024]{1,0:T(8,128)(2,1)} %q_hbm.1, ...), custom_call_target="tpu_custom_call" | custom-call | tf_op jit(solution)/shard_map/prepare/pallas_call | solution.py:329
  4.2 0.0 copy-start.1
  4.2 7.7 %all-to-all-start = ((bf16[8,384,128]{2,1,0:T(8,128)(2,1)}), bf16[8,384,128]{2,1,0:T(8,128)(2,1)S(1)}, u32[]{:S(2)}, u32[]{:S(2)}) async-start(bf16[8,384,128]{2,1,0:T(8,128)(2,1)} %get-tuple-element.9), calls=%async_computation | async-start | bytes 1572864 | tf_op jit(solution)/shard_map/all_to_all | solution.py:359
  11.9 0.0 copy-done.1
  11.9 22.0 %all_gather.6.own_ref = bf16[1280,256]{1,0:T(8,128)(2,1)S(1)} all-gather(bf16[320,256]{1,0:T(8,128)(2,1)S(1)} %copy-done.1), channel_id=1, replica_groups={{0,128,256,384},{8,136,264,392},{16,144,272,400},{24,152,280,408},{32,1..., dimensions={0}, use_global_device_ids=true | all-gather | bytes 819200 | tf_op jit(solution)/shard_map/all_gather | solution.py:362
  33.8 0.0 copy-start
  33.8 2.0 %collective-permute-start = (bf16[1280,256]{1,0:T(8,128)(2,1)S(1)}, bf16[1280,256]{1,0:T(8,128)(2,1)S(1)}, u32[]{:S(2)}, u32[]{:S(2)}) collective-permute-start(bf16[1280,256]{1,0:T(8,128)(2,1)S(1)} %all_gather.6.own_ref), channel_id=1, source_target_pairs={{0,8},{8,0},{16,24},{24,16},{32,40},{40,32},{48,56},{56,48},{64,72... | collective-permute-start | bytes 1966088 | tf_op jit(solution)/shard_map/ppermute | solution.py:363
  35.9 2.1 %collective-permute-done.other_ref = bf16[1280,256]{1,0:T(8,128)(2,1)S(1)} collective-permute-done((bf16[1280,256]{1,0:T(8,128)(2,1)S(1)}, bf16[1280,256]{1,0:T(8,128)(2,1)S(1)}, u32[]{:S(2)}, u32[]{:S(2)}) %collective-permute-start) | collective-permute-done | bytes 655392 | tf_op jit(solution)/shard_map/ppermute | solution.py:363
  37.9 0.0 all-to-all-done
  37.9 0.0 copy-done
  37.9 9.7 %attend.1 = bf16[8,136,384]{2,1,0:T(8,128)(2,1)} custom-call(s32[1,48]{1,0:T(1,128)S(1)} %copy-done, bf16[3072,128]{1,0:T(8,128)(2,1)S(1)} %bitcast.6, bf16[1280,256]{1,0:T(8,128)(2,1)S(1)} %all_gather.6.own_ref, bf16[1280,256]{1,0:T(8,128)(2,1)S(1)} %collective-permute-done.other_ref), custom_call_target="tpu_custom_call" | custom-call | tf_op jit(solution)/shard_map/attend/pallas_call | solution.py:366
  47.6 8.3 %all-to-all-start.1 = ((bf16[8,136,384]{2,1,0:T(8,128)(2,1)}), bf16[8,136,384]{2,1,0:T(8,128)(2,1)S(1)}, u32[]{:S(2)}, u32[]{:S(2)}) async-start(bf16[8,136,384]{2,1,0:T(8,128)(2,1)} %attend.1), calls=%async_computation.1 | async-start | bytes 1671168 | tf_op jit(solution)/shard_map/all_to_all | solution.py:386
  56.0 0.0 copy-start.2
  56.0 0.7 copy-done.2
  56.6 14.2 %all-gather = f32[8,1,48]{2,1,0:T(1,128)S(1)} all-gather(f32[1,1,48]{2,1,0:T(1,128)S(1)} %bitcast.7), channel_id=1, replica_groups=mesh['ctx'=64,'head'=8] {'head'}, dimensions={0}, use_global_device_ids=true | all-gather | bytes 1728 | tf_op jit(solution)/shard_map/all_gather | solution.py:389
  70.8 0.5 compare_select_fusion
  71.3 5.5 %all-to-all-done.1.parts_ref = bf16[8,136,384]{2,1,0:T(8,128)(2,1)S(1)} async-done(((bf16[8,136,384]{2,1,0:T(8,128)(2,1)}), bf16[8,136,384]{2,1,0:T(8,128)(2,1)S(1)}, u32[]{:S(2)}, u32[]{:S(2)}) %all-to-all-start.1) | async-done | bytes 835616 | tf_op jit(solution)/shard_map/all_to_all | solution.py:386
  76.9 0.9 %merge.1 = bf16[48,1024]{1,0:T(8,128)(2,1)} custom-call(s32[1]{0:T(128)} %copy.12.count_ref, bf16[8,136,384]{2,1,0:T(8,128)(2,1)S(1)} %all-to-all-done.1.parts_ref), custom_call_target="tpu_custom_call" | custom-call | tf_op jit(solution)/shard_map/merge/pallas_call | solution.py:394
  (1 shorter events, 0.0 us)
Async XLA Ops:
  4.2 7.7 %copy-start.1 = (bf16[320,256]{1,0:T(8,128)(2,1)S(1)}, bf16[320,256]{1,0:T(8,128)(2,1)}, u32[]{:S(2)}) copy-start(bf16[320,256]{1,0:T(8,128)(2,1)} %get-tuple-element.10) | copy-start | bytes 491524
  4.2 33.8 %all-to-all-start = ((bf16[8,384,128]{2,1,0:T(8,128)(2,1)}), bf16[8,384,128]{2,1,0:T(8,128)(2,1)S(1)}, u32[]{:S(2)}, u32[]{:S(2)}) async-start(bf16[8,384,128]{2,1,0:T(8,128)(2,1)} %get-tuple-element.9), calls=%async_computation | async-start | bytes 1572864 | tf_op jit(solution)/shard_map/all_to_all | solution.py:359
  33.8 4.1 %copy-start = (s32[1,48]{1,0:T(1,128)S(1)}, s32[1,48]{1,0:T(1,128)}, u32[]{:S(2)}) copy-start(s32[1,48]{1,0:T(1,128)} %index_ref.1) | copy-start | bytes 580
  33.8 4.1 %collective-permute-start = (bf16[1280,256]{1,0:T(8,128)(2,1)S(1)}, bf16[1280,256]{1,0:T(8,128)(2,1)S(1)}, u32[]{:S(2)}, u32[]{:S(2)}) collective-permute-start(bf16[1280,256]{1,0:T(8,128)(2,1)S(1)} %all_gather.6.own_ref), channel_id=1, source_target_pairs={{0,8},{8,0},{16,24},{24,16},{32,40},{40,32},{48,56},{56,48},{64,72... | collective-permute-start | bytes 1966088 | tf_op jit(solution)/shard_map/ppermute | solution.py:363
  47.6 29.2 %all-to-all-start.1 = ((bf16[8,136,384]{2,1,0:T(8,128)(2,1)}), bf16[8,136,384]{2,1,0:T(8,128)(2,1)S(1)}, u32[]{:S(2)}, u32[]{:S(2)}) async-start(bf16[8,136,384]{2,1,0:T(8,128)(2,1)} %attend.1), calls=%async_computation.1 | async-start | bytes 1671168 | tf_op jit(solution)/shard_map/all_to_all | solution.py:386
  56.0 0.7 copy-start.2

commit v6 on v5

--- a/solution.py
+++ b/solution.py
@@ -29,7 +29,6 @@
 SCORE_SCALE = 1.0 / math.sqrt(HEAD_DIM)
 
 VMEM = pl.BlockSpec(memory_space=pltpu.VMEM)
-SMEM = pl.BlockSpec(memory_space=pltpu.SMEM)
 HBM = pl.BlockSpec(memory_space=pltpu.HBM)
 
 
@@ -71,15 +70,16 @@
 
 
 def prepare_kernel(
-    offsets, count_ref, index_hbm, q_hbm, ck_hbm, cv_hbm, fk_hbm, fv_hbm,
+    offsets_hbm, count_hbm, index_hbm, q_hbm, ck_hbm, cv_hbm, fk_hbm, fv_hbm,
     q_out, kv_out, jk_out, jv_out, drift_out,
-    index_ref, q_ref, ck_ref, cv_ref, fk_ref, fv_ref, copies_ref, kv_ref, drift_ref, arrived, left,
+    offsets_ref, count_ref, index_ref, q_ref, ck_ref, cv_ref, fk_ref, fv_ref, copies_ref, kv_ref, drift_ref,
+    arrived, left,
 ):
     copies = [
         pltpu.make_async_copy(source, target, arrived.at[i])
         for i, (source, target) in enumerate((
-            (index_hbm, index_ref), (q_hbm, q_ref), (fk_hbm, fk_ref),
-            (ck_hbm, ck_ref), (fv_hbm, fv_ref), (cv_hbm, cv_ref),
+            (offsets_hbm, offsets_ref), (count_hbm, count_ref), (index_hbm, index_ref),
+            (q_hbm, q_ref), (fk_hbm, fk_ref), (ck_hbm, ck_ref), (fv_hbm, fv_ref), (cv_hbm, cv_ref),
         ))
     ]
     for copy in copies:
@@ -99,14 +99,21 @@
     freq = jnp.zeros((1, HEAD_DIM), jnp.float32)
     for i, value in enumerate(inverse_freq()):
         freq = jnp.where(lane == i, value, freq)
-    own_start = offsets[lax.axis_index("ctx")]
-    count = count_ref[0]
-    copies[0].wait()
+    for copy in copies[:3]:
+        copy.wait()
+    groups = offsets_ref.shape[1]
+    own_start = jnp.sum(
+        jnp.where(
+            iota((1, groups), 1) == lax.axis_index("ctx"), offsets_ref[...].astype(jnp.float32), 0.0
+        ),
+        axis=1,
+        keepdims=True,
+    )
+    count = count_ref[...]
     index_row = index_ref[...]
     index_col = column_of(index_row.astype(jnp.float32))
-    start_row = jnp.full((1, HEAD_DIM), own_start, jnp.int32).astype(jnp.float32)
-    slot_angle = (index_col + start_row[:, :1]) * freq
-    group_angle = start_row * freq
+    slot_angle = (index_col + own_start) * freq
+    group_angle = own_start * freq
     sign = jnp.where(iota((1, HEAD_DIM), 1) < half, -1.0, 1.0)
     slot_cos, slot_sin = jnp.cos(slot_angle), jnp.sin(slot_angle) * sign
     group_cos, group_sin = jnp.cos(group_angle), jnp.sin(group_angle) * sign
@@ -115,14 +122,14 @@
         x = rows.astype(jnp.float32)
         return (x * cosine + pltpu.roll(x, half, 1) * sine).astype(jnp.bfloat16)
 
-    copies[1].wait()
+    copies[3].wait()
     for h in range(HEADS_PER):
         head = turn(q_ref[:, h * HEAD_DIM : (h + 1) * HEAD_DIM], slot_cos, slot_sin)
         for y in range(Y):
             copies_ref[y, h * SLOTS : (h + 1) * SLOTS, :] = head
     sends[0].start()
 
-    for copy in copies[2:]:
+    for copy in copies[4:]:
         copy.wait()
     turned = turn(ck_ref[...], group_cos, group_sin)
     fresh = turn(fk_ref[...], slot_cos, slot_sin)
@@ -287,7 +294,7 @@
 
 
 def merge_kernel(count_ref, parts_ref, out_ref):
-    live = iota((SLOTS, HEAD_DIM), 0) < count_ref[0]
+    live = iota((SLOTS, HEAD_DIM), 0) < count_ref[...]
     levels = []
     for y in range(Y):
         stat = parts_ref[y, HEAD_DIM:, :].astype(jnp.float32)
@@ -326,6 +333,7 @@
 ):
     bf16, f32 = jnp.bfloat16, jnp.float32
     shape = jax.ShapeDtypeStruct
+    count = recompute_count.reshape(1, 1)
     copies, own_kv, joined_keys, joined_values, squares = pl.pallas_call(
         prepare_kernel,
         out_shape=(
@@ -335,9 +343,11 @@
             shape((GROUP_LEN, HEAD_DIM), bf16),
             shape((1, SLOTS), f32),
         ),
-        in_specs=[SMEM, SMEM] + [HBM] * 6,
+        in_specs=[HBM] * 8,
         out_specs=[HBM] * 5,
         scratch_shapes=[
+            pltpu.VMEM((1, group_offsets.shape[0]), jnp.int32),
+            pltpu.VMEM((1, 1), jnp.int32),
             pltpu.VMEM((1, SLOTS), jnp.int32),
             pltpu.VMEM((SLOTS, HEADS_PER * HEAD_DIM), bf16),
             pltpu.VMEM((GROUP_LEN, HEAD_DIM), bf16),
@@ -347,12 +357,12 @@
             pltpu.VMEM((Y, ROWS, HEAD_DIM), bf16),
             pltpu.VMEM((GROUP_LEN, 2 * HEAD_DIM), bf16),
             pltpu.VMEM((1, SLOTS), f32),
-            pltpu.SemaphoreType.DMA((6,)),
+            pltpu.SemaphoreType.DMA((8,)),
             pltpu.SemaphoreType.DMA((5,)),
         ],
         name="prepare",
     )(
-        group_offsets, recompute_count, recompute_index,
+        group_offsets.reshape(1, -1), count, recompute_index,
         queries, cached_keys, cached_values, fresh_keys, fresh_values,
     )
 
@@ -394,11 +404,11 @@
     attention = pl.pallas_call(
         merge_kernel,
         out_shape=shape((SLOTS, HEADS_PER * HEAD_DIM), bf16),
-        in_specs=[SMEM, VMEM],
+        in_specs=[VMEM, VMEM],
         out_specs=VMEM,
         compiler_params=kernel_params(16),
         name="merge",
-    )(recompute_count, parts)
+    )(count, parts)
     return (attention, joined_keys, joined_values, drift)
 
 

time: 78.1 us -> 77.5 us (level)
  the two profiles are of different devices: /device:TPU:76 before, /device:TPU:78 now
where the time goes in v6:
time: 77.5 us; the launch traced here: 77.2 us
  blocking collectives  36.8 us (47%)
  starting transfers between devices  18.1 us (23%)
  Pallas kernels  12.8 us (17%)
  waiting for transfers between devices  6.95 us (9%)
  between operations  1.32 us (2%)
    all_gather x1, blocking collectives, shards(): lax.all_gather(own_kv, 'ctx', axis=0, axis_index_groups=KEY_GROUPS, tiled...  22 us
    all_gather x1, blocking collectives, shards(): squares = lax.all_gather(squares, 'head', axis=0, tiled=True)  14.8 us
    pallas_call x1, Pallas kernels, shards(): pl.pallas_call(attend_kernel, out_shape=shape((Y, HEAD_DIM + STAT_ROWS, R...  9.66 us
    all_to_all x1, starting transfers between devices, shards(): lax.all_to_all(partial, 'ctx', 0, 0, axis_index_groups=QUERY_GROUPS, tile...  8.34 us
    all_to_all x1, starting transfers between devices, shards(): lax.all_to_all(copies, 'ctx', 0, 0, axis_index_groups=QUERY_GROUPS, tiled...  7.69 us
    all_to_all x1, waiting for transfers between devices, shards(): lax.all_to_all(partial, 'ctx', 0, 0, axis_index_groups=QUERY_GROUPS, tile...  4.88 us
    pallas_call x1, Pallas kernels, shards(): pl.pallas_call(prepare_kernel, out_shape=(shape((Y, ROWS, HEAD_DIM), bf16...  2.27 us
    ppermute x1, waiting for transfers between devices, shards(): other_kv = lax.ppermute(core_kv, 'ctx', CORE_SWAP)  2.06 us
  transfers between devices with their start and end apart: 3, of which 2 were waited for; matrix products, arithmetic and copies ran while one was open for 1% of the time, Pallas kernels for 0%

profile of v6, /device:TPU:78, one launch (start us, length us, event | category | flops | bytes accessed | tf_op | source)
XLA Modules:
  0.0 77.2 jit_solution(2759577042196401864)
XLA Ops:
  1.3 2.3 %prepare.1 = (bf16[8,384,128]{2,1,0:T(8,128)(2,1)}, bf16[320,256]{1,0:T(8,128)(2,1)}, bf16[320,128]{1,0:T(8,128)(2,1)}, bf16[320,128]{1,0:T(8,128)(2,1)}, f32[1,48]{1,0:T(1,128)}) custom-call(s32[1,64]{1,0:T(1,128)} %bitcast.11, s32[1,1]{1,0:T(1,128)} %bitcast.7.count_hbm, s32[1,48]{1,0:T(1,128)} %index_ref.1, bf16[48,1024]{1,0:T(8,128)(2,1)} %q_hbm.1, ...), custom_call_target="tpu_custom_call" | custom-call | tf_op jit(solution)/shard_map/prepare/pallas_call | solution.py:337
  3.6 0.0 copy-start.1
  3.6 7.7 %all-to-all-start = ((bf16[8,384,128]{2,1,0:T(8,128)(2,1)}), bf16[8,384,128]{2,1,0:T(8,128)(2,1)S(1)}, u32[]{:S(2)}, u32[]{:S(2)}) async-start(bf16[8,384,128]{2,1,0:T(8,128)(2,1)} %get-tuple-element.9), calls=%async_computation | async-start | bytes 1572864 | tf_op jit(solution)/shard_map/all_to_all | solution.py:369
  11.3 0.0 copy-done.1
  11.3 22.0 %all_gather.6.own_ref = bf16[1280,256]{1,0:T(8,128)(2,1)S(1)} all-gather(bf16[320,256]{1,0:T(8,128)(2,1)S(1)} %copy-done.1), channel_id=1, replica_groups={{0,128,256,384},{8,136,264,392},{16,144,272,400},{24,152,280,408},{32,1..., dimensions={0}, use_global_device_ids=true | all-gather | bytes 819200 | tf_op jit(solution)/shard_map/all_gather | solution.py:372
  33.2 0.0 copy-start
  33.2 2.0 %collective-permute-start = (bf16[1280,256]{1,0:T(8,128)(2,1)S(1)}, bf16[1280,256]{1,0:T(8,128)(2,1)S(1)}, u32[]{:S(2)}, u32[]{:S(2)}) collective-permute-start(bf16[1280,256]{1,0:T(8,128)(2,1)S(1)} %all_gather.6.own_ref), channel_id=1, source_target_pairs={{0,8},{8,0},{16,24},{24,16},{32,40},{40,32},{48,56},{56,48},{64,72... | collective-permute-start | bytes 1966088 | tf_op jit(solution)/shard_map/ppermute | solution.py:373
  35.3 2.1 %collective-permute-done.other_ref = bf16[1280,256]{1,0:T(8,128)(2,1)S(1)} collective-permute-done((bf16[1280,256]{1,0:T(8,128)(2,1)S(1)}, bf16[1280,256]{1,0:T(8,128)(2,1)S(1)}, u32[]{:S(2)}, u32[]{:S(2)}) %collective-permute-start) | collective-permute-done | bytes 655392 | tf_op jit(solution)/shard_map/ppermute | solution.py:373
  37.3 0.0 all-to-all-done
  37.3 0.0 copy-done
  37.4 9.7 %attend.1 = bf16[8,136,384]{2,1,0:T(8,128)(2,1)} custom-call(s32[1,48]{1,0:T(1,128)S(1)} %copy-done, bf16[3072,128]{1,0:T(8,128)(2,1)S(1)} %bitcast.10, bf16[1280,256]{1,0:T(8,128)(2,1)S(1)} %all_gather.6.own_ref, bf16[1280,256]{1,0:T(8,128)(2,1)S(1)} %collective-permute-done.other_ref), custom_call_target="tpu_custom_call" | custom-call | tf_op jit(solution)/shard_map/attend/pallas_call | solution.py:376
  47.0 8.3 %all-to-all-start.1 = ((bf16[8,136,384]{2,1,0:T(8,128)(2,1)}), bf16[8,136,384]{2,1,0:T(8,128)(2,1)S(1)}, u32[]{:S(2)}, u32[]{:S(2)}) async-start(bf16[8,136,384]{2,1,0:T(8,128)(2,1)} %attend.1), calls=%async_computation.1 | async-start | bytes 1671168 | tf_op jit(solution)/shard_map/all_to_all | solution.py:396
  55.4 0.0 copy-start.2
  55.4 0.7 copy-done.2
  56.0 14.8 %all-gather = f32[8,1,48]{2,1,0:T(1,128)S(1)} all-gather(f32[1,1,48]{2,1,0:T(1,128)S(1)} %bitcast.12), channel_id=1, replica_groups=mesh['ctx'=64,'head'=8] {'head'}, dimensions={0}, use_global_device_ids=true | all-gather | bytes 1728 | tf_op jit(solution)/shard_map/all_gather | solution.py:399
  70.9 0.5 compare_select_fusion
  71.4 4.9 %all-to-all-done.1.parts_ref = bf16[8,136,384]{2,1,0:T(8,128)(2,1)S(1)} async-done(((bf16[8,136,384]{2,1,0:T(8,128)(2,1)}), bf16[8,136,384]{2,1,0:T(8,128)(2,1)S(1)}, u32[]{:S(2)}, u32[]{:S(2)}) %all-to-all-start.1) | async-done | bytes 835616 | tf_op jit(solution)/shard_map/all_to_all | solution.py:396
  76.3 0.9 %merge.1 = bf16[48,1024]{1,0:T(8,128)(2,1)} custom-call(s32[1,1]{1,0:T(1,128)} %bitcast.8.count_ref, bf16[8,136,384]{2,1,0:T(8,128)(2,1)S(1)} %all-to-all-done.1.parts_ref), custom_call_target="tpu_custom_call" | custom-call | tf_op jit(solution)/shard_map/merge/pallas_call | solution.py:404
  (1 shorter events, 0.0 us)
Async XLA Ops:
  3.6 7.7 %copy-start.1 = (bf16[320,256]{1,0:T(8,128)(2,1)S(1)}, bf16[320,256]{1,0:T(8,128)(2,1)}, u32[]{:S(2)}) copy-start(bf16[320,256]{1,0:T(8,128)(2,1)} %get-tuple-element.10) | copy-start | bytes 491524
  3.6 33.8 %all-to-all-start = ((bf16[8,384,128]{2,1,0:T(8,128)(2,1)}), bf16[8,384,128]{2,1,0:T(8,128)(2,1)S(1)}, u32[]{:S(2)}, u32[]{:S(2)}) async-start(bf16[8,384,128]{2,1,0:T(8,128)(2,1)} %get-tuple-element.9), calls=%async_computation | async-start | bytes 1572864 | tf_op jit(solution)/shard_map/all_to_all | solution.py:369
  33.2 4.1 %copy-start = (s32[1,48]{1,0:T(1,128)S(1)}, s32[1,48]{1,0:T(1,128)}, u32[]{:S(2)}) copy-start(s32[1,48]{1,0:T(1,128)} %index_ref.1) | copy-start | bytes 580
  33.2 4.1 %collective-permute-start = (bf16[1280,256]{1,0:T(8,128)(2,1)S(1)}, bf16[1280,256]{1,0:T(8,128)(2,1)S(1)}, u32[]{:S(2)}, u32[]{:S(2)}) collective-permute-start(bf16[1280,256]{1,0:T(8,128)(2,1)S(1)} %all_gather.6.own_ref), channel_id=1, source_target_pairs={{0,8},{8,0},{16,24},{24,16},{32,40},{40,32},{48,56},{56,48},{64,72... | collective-permute-start | bytes 1966088 | tf_op jit(solution)/shard_map/ppermute | solution.py:373
  47.0 29.2 %all-to-all-start.1 = ((bf16[8,136,384]{2,1,0:T(8,128)(2,1)}), bf16[8,136,384]{2,1,0:T(8,128)(2,1)S(1)}, u32[]{:S(2)}, u32[]{:S(2)}) async-start(bf16[8,136,384]{2,1,0:T(8,128)(2,1)} %attend.1), calls=%async_computation.1 | async-start | bytes 1671168 | tf_op jit(solution)/shard_map/all_to_all | solution.py:396
  55.4 0.7 copy-start.2

commit v7 on v6

--- a/solution.py
+++ b/solution.py
@@ -36,7 +36,7 @@
     return (z_hi * Y + y) * CORES + core
 
 
-QUERY_ORDERS = [list(range(Y)), list(range(Y - 1, -1, -1))]
+QUERY_ORDERS = [[7, 0, 6, 1, 5, 2, 4, 3]] * CORES
 QUERY_GROUPS = [
     [ctx_index(z, y, c) for y in QUERY_ORDERS[c]] for z in range(Z_HI) for c in range(CORES)
 ]
@@ -396,9 +396,10 @@
     parts = lax.all_to_all(
         partial, "ctx", 0, 0, axis_index_groups=QUERY_GROUPS, tiled=True
     )
-    squares = lax.all_gather(squares, "head", axis=0, tiled=True)
-    drift = squares.sum(axis=0, keepdims=True)
-    drift = drift / (2.0 * KV_HEADS * HEAD_DIM)
+    for step in (1, 2):
+        squares = squares + lax.ppermute(squares, "head", [(i, i ^ step) for i in range(KV_HEADS)])
+    other = lax.ppermute(squares, "head", [(i, i ^ 4) for i in range(KV_HEADS)])
+    drift = (squares + other) / (2.0 * KV_HEADS * HEAD_DIM)
     drift = jnp.where(iota((1, SLOTS), 1) < recompute_count[0], drift, 0.0)
 
     attention = pl.pallas_call(

time: 77.5 us -> 77.4 us (level)
  the two profiles are of different devices: /device:TPU:78 before, /device:TPU:1 now
where the time goes in v7:
time: 77.4 us; the launch traced here: 77 us
  starting transfers between devices  30.9 us (40%)
  blocking collectives  20.5 us (26%)
  Pallas kernels  12.9 us (17%)
  waiting for transfers between devices  10.2 us (13%)
  between operations  1.34 us (2%)
    all_gather x1, blocking collectives, shards(): lax.all_gather(own_kv, 'ctx', axis=0, axis_index_groups=KEY_GROUPS, tiled...  20.5 us
    pallas_call x1, Pallas kernels, shards(): pl.pallas_call(attend_kernel, out_shape=shape((Y, HEAD_DIM + STAT_ROWS, R...  9.69 us
    all_to_all x1, starting transfers between devices, shards(): lax.all_to_all(copies, 'ctx', 0, 0, axis_index_groups=QUERY_GROUPS, tiled...  8.07 us
    ppermute x2, starting transfers between devices, shards(): lax.ppermute(squares, 'head', [(i, i ^ step) for i in range(KV_HEADS)])  7.49 us
    all_to_all x1, starting transfers between devices, shards(): lax.all_to_all(partial, 'ctx', 0, 0, axis_index_groups=QUERY_GROUPS, tile...  6.5 us
    ppermute x1, starting transfers between devices, shards(): other_kv = lax.ppermute(core_kv, 'ctx', CORE_SWAP)  5.73 us
    all_to_all x1, waiting for transfers between devices, shards(): lax.all_to_all(partial, 'ctx', 0, 0, axis_index_groups=QUERY_GROUPS, tile...  3.86 us
    ppermute x2, waiting for transfers between devices, shards(): lax.ppermute(squares, 'head', [(i, i ^ step) for i in range(KV_HEADS)])  3.19 us
  transfers between devices with their start and end apart: 6, of which 5 were waited for; matrix products, arithmetic and copies ran while one was open for 1% of the time, Pallas kernels for 0%

profile of v7, /device:TPU:1, one launch (start us, length us, event | category | flops | bytes accessed | tf_op | source)
XLA Modules:
  0.0 77.0 jit_solution(6711976465020214081)
XLA Ops:
  1.3 2.3 %prepare.1 = (bf16[8,384,128]{2,1,0:T(8,128)(2,1)}, bf16[320,256]{1,0:T(8,128)(2,1)}, bf16[320,128]{1,0:T(8,128)(2,1)}, bf16[320,128]{1,0:T(8,128)(2,1)}, f32[1,48]{1,0:T(1,128)}) custom-call(s32[1,64]{1,0:T(1,128)} %bitcast.8, s32[1,1]{1,0:T(1,128)} %bitcast.4.count_hbm, s32[1,48]{1,0:T(1,128)} %index_ref.1, bf16[48,1024]{1,0:T(8,128)(2,1)} %q_hbm.1, ...), custom_call_target="tpu_custom_call" | custom-call | tf_op jit(solution)/shard_map/prepare/pallas_call | solution.py:337
  3.6 0.0 copy-start.1
  3.6 8.1 %all-to-all-start = ((bf16[8,384,128]{2,1,0:T(8,128)(2,1)}), bf16[8,384,128]{2,1,0:T(8,128)(2,1)S(1)}, u32[]{:S(2)}, u32[]{:S(2)}) async-start(bf16[8,384,128]{2,1,0:T(8,128)(2,1)} %get-tuple-element.9), calls=%async_computation | async-start | bytes 1572864 | tf_op jit(solution)/shard_map/all_to_all | solution.py:369
  11.6 0.0 copy-done.1
  11.6 20.5 %all_gather.3.own_ref = bf16[1280,256]{1,0:T(8,128)(2,1)S(1)} all-gather(bf16[320,256]{1,0:T(8,128)(2,1)S(1)} %copy-done.1), channel_id=1, replica_groups={{0,128,256,384},{8,136,264,392},{16,144,272,400},{24,152,280,408},{32,1..., dimensions={0}, use_global_device_ids=true | all-gather | bytes 819200 | tf_op jit(solution)/shard_map/all_gather | solution.py:372
  32.1 0.0 copy-start
  32.1 5.7 %collective-permute-start = (bf16[1280,256]{1,0:T(8,128)(2,1)S(1)}, bf16[1280,256]{1,0:T(8,128)(2,1)S(1)}, u32[]{:S(2)}, u32[]{:S(2)}) collective-permute-start(bf16[1280,256]{1,0:T(8,128)(2,1)S(1)} %all_gather.3.own_ref), channel_id=1, source_target_pairs={{0,8},{8,0},{16,24},{24,16},{32,40},{40,32},{48,56},{56,48},{64,72... | collective-permute-start | bytes 1966088 | tf_op jit(solution)/shard_map/ppermute | solution.py:373
  37.9 1.7 %collective-permute-done.other_ref = bf16[1280,256]{1,0:T(8,128)(2,1)S(1)} collective-permute-done((bf16[1280,256]{1,0:T(8,128)(2,1)S(1)}, bf16[1280,256]{1,0:T(8,128)(2,1)S(1)}, u32[]{:S(2)}, u32[]{:S(2)}) %collective-permute-start) | collective-permute-done | bytes 655392 | tf_op jit(solution)/shard_map/ppermute | solution.py:373
  39.6 0.0 all-to-all-done
  39.6 0.0 copy-done
  39.6 9.7 %attend.1 = bf16[8,136,384]{2,1,0:T(8,128)(2,1)} custom-call(s32[1,48]{1,0:T(1,128)S(1)} %copy-done, bf16[3072,128]{1,0:T(8,128)(2,1)S(1)} %bitcast.7, bf16[1280,256]{1,0:T(8,128)(2,1)S(1)} %all_gather.3.own_ref, bf16[1280,256]{1,0:T(8,128)(2,1)S(1)} %collective-permute-done.other_ref), custom_call_target="tpu_custom_call" | custom-call | tf_op jit(solution)/shard_map/attend/pallas_call | solution.py:376
  49.3 6.5 %all-to-all-start.1 = ((bf16[8,136,384]{2,1,0:T(8,128)(2,1)}), bf16[8,136,384]{2,1,0:T(8,128)(2,1)S(1)}, u32[]{:S(2)}, u32[]{:S(2)}) async-start(bf16[8,136,384]{2,1,0:T(8,128)(2,1)} %attend.1), calls=%async_computation.1 | async-start | bytes 1671168 | tf_op jit(solution)/shard_map/all_to_all | solution.py:396
  55.8 0.0 copy-start.2
  55.8 0.7 copy-done.2
  56.4 3.1 %collective-permute-start.1 = (f32[1,48]{1,0:T(1,128)S(1)}, f32[1,48]{1,0:T(1,128)S(1)}, u32[]{:S(2)}, u32[]{:S(2)}) collective-permute-start(f32[1,48]{1,0:T(1,128)S(1)} %copy-done.2), channel_id=1, source_target_pairs={{0,1},{1,0},{2,3},{3,2},{4,5},{5,4},{6,7},{7,6},{8,9},{9,8},{10,11... | collective-permute-start | bytes 584 | tf_op jit(solution)/shard_map/ppermute | solution.py:400
  59.5 1.5 %collective-permute-done.1 = f32[1,48]{1,0:T(1,128)S(1)} collective-permute-done((f32[1,48]{1,0:T(1,128)S(1)}, f32[1,48]{1,0:T(1,128)S(1)}, u32[]{:S(2)}, u32[]{:S(2)}) %collective-permute-start.1) | collective-permute-done | bytes 224 | tf_op jit(solution)/shard_map/ppermute | solution.py:400
  61.0 4.4 %collective-permute-start.2 = (f32[1,48]{1,0:T(1,128)S(1)}, f32[1,48]{1,0:T(1,128)S(1)}, u32[]{:S(2)}, u32[]{:S(2)}) collective-permute-start(f32[1,48]{1,0:T(1,128)S(1)} %add.9), channel_id=1, source_target_pairs={{0,2},{1,3},{2,0},{3,1},{4,6},{5,7},{6,4},{7,5},{8,10},{9,11},{10,... | collective-permute-start | bytes 584 | tf_op jit(solution)/shard_map/ppermute | solution.py:400
  65.4 1.7 %collective-permute-done.2 = f32[1,48]{1,0:T(1,128)S(1)} collective-permute-done((f32[1,48]{1,0:T(1,128)S(1)}, f32[1,48]{1,0:T(1,128)S(1)}, u32[]{:S(2)}, u32[]{:S(2)}) %collective-permute-start.2) | collective-permute-done | bytes 224 | tf_op jit(solution)/shard_map/ppermute | solution.py:400
  67.1 3.1 %collective-permute-start.3 = (f32[1,48]{1,0:T(1,128)S(1)}, f32[1,48]{1,0:T(1,128)S(1)}, u32[]{:S(2)}, u32[]{:S(2)}) collective-permute-start(f32[1,48]{1,0:T(1,128)S(1)} %add.10), channel_id=1, source_target_pairs={{0,4},{1,5},{2,6},{3,7},{4,0},{5,1},{6,2},{7,3},{8,12},{9,13},{10,... | collective-permute-start | bytes 584 | tf_op jit(solution)/shard_map/ppermute | solution.py:401
  70.3 1.5 %collective-permute-done.3 = f32[1,48]{1,0:T(1,128)S(1)} collective-permute-done((f32[1,48]{1,0:T(1,128)S(1)}, f32[1,48]{1,0:T(1,128)S(1)}, u32[]{:S(2)}, u32[]{:S(2)}) %collective-permute-start.3) | collective-permute-done | bytes 224 | tf_op jit(solution)/shard_map/ppermute | solution.py:401
  71.7 0.5 compare_select_fusion
  72.3 3.9 %all-to-all-done.1.parts_ref = bf16[8,136,384]{2,1,0:T(8,128)(2,1)S(1)} async-done(((bf16[8,136,384]{2,1,0:T(8,128)(2,1)}), bf16[8,136,384]{2,1,0:T(8,128)(2,1)S(1)}, u32[]{:S(2)}, u32[]{:S(2)}) %all-to-all-start.1) | async-done | bytes 835616 | tf_op jit(solution)/shard_map/all_to_all | solution.py:396
  76.1 0.9 %merge.1 = bf16[48,1024]{1,0:T(8,128)(2,1)} custom-call(s32[1,1]{1,0:T(1,128)} %bitcast.5.count_ref, bf16[8,136,384]{2,1,0:T(8,128)(2,1)S(1)} %all-to-all-done.1.parts_ref), custom_call_target="tpu_custom_call" | custom-call | tf_op jit(solution)/shard_map/merge/pallas_call | solution.py:405
  (2 shorter events, 0.0 us)
Async XLA Ops:
  3.6 8.1 %copy-start.1 = (bf16[320,256]{1,0:T(8,128)(2,1)S(1)}, bf16[320,256]{1,0:T(8,128)(2,1)}, u32[]{:S(2)}) copy-start(bf16[320,256]{1,0:T(8,128)(2,1)} %get-tuple-element.10) | copy-start | bytes 491524
  3.6 36.0 %all-to-all-start = ((bf16[8,384,128]{2,1,0:T(8,128)(2,1)}), bf16[8,384,128]{2,1,0:T(8,128)(2,1)S(1)}, u32[]{:S(2)}, u32[]{:S(2)}) async-start(bf16[8,384,128]{2,1,0:T(8,128)(2,1)} %get-tuple-element.9), calls=%async_computation | async-start | bytes 1572864 | tf_op jit(solution)/shard_map/all_to_all | solution.py:369
  32.1 7.4 %copy-start = (s32[1,48]{1,0:T(1,128)S(1)}, s32[1,48]{1,0:T(1,128)}, u32[]{:S(2)}) copy-start(s32[1,48]{1,0:T(1,128)} %index_ref.1) | copy-start | bytes 580
  32.1 7.4 %collective-permute-start = (bf16[1280,256]{1,0:T(8,128)(2,1)S(1)}, bf16[1280,256]{1,0:T(8,128)(2,1)S(1)}, u32[]{:S(2)}, u32[]{:S(2)}) collective-permute-start(bf16[1280,256]{1,0:T(8,128)(2,1)S(1)} %all_gather.3.own_ref), channel_id=1, source_target_pairs={{0,8},{8,0},{16,24},{24,16},{32,40},{40,32},{48,56},{56,48},{64,72... | collective-permute-start | bytes 1966088 | tf_op jit(solution)/shard_map/ppermute | solution.py:373
  49.3 26.8 %all-to-all-start.1 = ((bf16[8,136,384]{2,1,0:T(8,128)(2,1)}), bf16[8,136,384]{2,1,0:T(8,128)(2,1)S(1)}, u32[]{:S(2)}, u32[]{:S(2)}) async-start(bf16[8,136,384]{2,1,0:T(8,128)(2,1)} %attend.1), calls=%async_computation.1 | async-start | bytes 1671168 | tf_op jit(solution)/shard_map/all_to_all | solution.py:396
  55.8 0.7 copy-start.2
  56.4 4.6 %collective-permute-start.1 = (f32[1,48]{1,0:T(1,128)S(1)}, f32[1,48]{1,0:T(1,128)S(1)}, u32[]{:S(2)}, u32[]{:S(2)}) collective-permute-start(f32[1,48]{1,0:T(1,128)S(1)} %copy-done.2), channel_id=1, source_target_pairs={{0,1},{1,0},{2,3},{3,2},{4,5},{5,4},{6,7},{7,6},{8,9},{9,8},{10,11... | collective-permute-start | bytes 584 | tf_op jit(solution)/shard_map/ppermute | solution.py:400
  61.0 6.1 %collective-permute-start.2 = (f32[1,48]{1,0:T(1,128)S(1)}, f32[1,48]{1,0:T(1,128)S(1)}, u32[]{:S(2)}, u32[]{:S(2)}) collective-permute-start(f32[1,48]{1,0:T(1,128)S(1)} %add.9), channel_id=1, source_target_pairs={{0,2},{1,3},{2,0},{3,1},{4,6},{5,7},{6,4},{7,5},{8,10},{9,11},{10,... | collective-permute-start | bytes 584 | tf_op jit(solution)/shard_map/ppermute | solution.py:400
  67.1 4.6 %collective-permute-start.3 = (f32[1,48]{1,0:T(1,128)S(1)}, f32[1,48]{1,0:T(1,128)S(1)}, u32[]{:S(2)}, u32[]{:S(2)}) collective-permute-start(f32[1,48]{1,0:T(1,128)S(1)} %add.10), channel_id=1, source_target_pairs={{0,4},{1,5},{2,6},{3,7},{4,0},{5,1},{6,2},{7,3},{8,12},{9,13},{10,... | collective-permute-start | bytes 584 | tf_op jit(solution)/shard_map/ppermute | solution.py:401
